TPU v7x, 32 devices: a whole 2x2x4 slice. The times are simulated.
32 devices in a mesh: tile: 16 (over z, y, core), band: 2 (over x).
Axes of the slice: x: 2, y: 2, z: 4, core: 2. Of those that a mesh axis runs over, the one named last changes fastest.
Arguments:
- stamps: bfloat16 [4096, 64, 128], P(('band', 'tile')), parts along dimension 0, may hold values from -6 to 6
- tile_of: int32 [4096, 1], P(('band', 'tile')), parts along dimension 0, may hold values from 0 to 15; in each aligned block of 128 rows (0 to 127, 128 to 255, ...) at most 10 rows name the same one
- row_offset: int32 [4096], P(('band', 'tile')), parts along dimension 0, may hold values from 0 to 7
- col_offset: int32 [4096], P(('band', 'tile')), parts along dimension 0, may hold values from 0 to 3
- psf_model: int32 [4096], P(('band', 'tile')), parts along dimension 0, may hold values from 0 to 17
- psf_rows: float32 [36, 3, 15], P('band'), parts along dimension 0, may hold values from -1.5 to 1.5
- psf_cols: float32 [36, 3, 15], P('band'), parts along dimension 0, may hold values from -1.5 to 1.5
- cotangent: bfloat16 [8192, 512], P(('band', 'tile')), parts along dimension 0, may hold values from -6 to 6
Outputs:
- tile_image: bfloat16 [8192, 512], P(('band', 'tile')), parts along dimension 0
- stamp_grad: bfloat16 [4096, 64, 128], P(('band', 'tile')), parts along dimension 0
There are 2 independent parts, one for each index of `band`. A program takes and returns all parts, laid end to end along the dimension named above; each array names one. Nothing has to cross between parts.
Inputs may be any that keep to these rules, and one draw needn't show every extreme that they name: `tile_of`: at most 10 of the stamps of one device lie on one tile, and in every draw some device places exactly 10 stamps on some tile.
All inputs are finite; a program needn't handle non-finite values.
Results may differ from a plain program's by a relative error of at most 0.007.
Values may be sent and summed in bfloat16 or wider, within the bound.
A program may use at most 128 MiB of HBM per device.

v0:
```python
from functools import partial

import jax
import jax.numpy as jnp
from jax import lax
from jax.sharding import PartitionSpec as P


def passed_along(array, axis, by):
    peers = lax.axis_size(axis)
    pairs = [(i, i + by) for i in range(peers) if 0 <= i + by < peers]
    return lax.ppermute(array, axis, pairs)


def for_sending(array):

    def short(part):
        return part.astype(jnp.bfloat16) if part.dtype == jnp.float32 else part

    return jax.tree.map(short, array)


def band_table(taps_count, size):
    half_width = (taps_count - 1) // 2
    places = jnp.arange(size, dtype=jnp.int32)
    offsets = places[None, :] - places[:, None] + half_width
    taps_index = jnp.arange(taps_count, dtype=jnp.int32)
    table = (offsets[None, :, :] == taps_index[:, None, None]).astype(jnp.float32)
    return table.reshape((taps_count, size * size))


def build_ops(profiles, size):
    model_total, term_total, taps_count = profiles.shape
    table = band_table(taps_count, size)
    mats = jnp.dot(
        profiles.reshape((model_total * term_total, taps_count)),
        table,
        precision=lax.Precision.HIGHEST,
    )
    return mats.reshape((model_total, term_total, size, size)).astype(jnp.bfloat16)


def convolve_one(inputs, row_ops, col_ops):
    image, model = inputs
    row_mats = lax.dynamic_index_in_dim(row_ops, model, 0, keepdims=False)
    col_mats = lax.dynamic_index_in_dim(col_ops, model, 0, keepdims=False)
    row_pass = jnp.einsum(
        "kij,jx->kix", row_mats, image, preferred_element_type=jnp.float32
    ).astype(jnp.bfloat16)
    return jnp.einsum("kix,kyx->iy", row_pass, col_mats, preferred_element_type=jnp.float32).astype(
        jnp.bfloat16
    )


def transpose_one(inputs, row_ops, col_ops):
    window, model = inputs
    row_mats = lax.dynamic_index_in_dim(row_ops, model, 0, keepdims=False)
    col_mats = lax.dynamic_index_in_dim(col_ops, model, 0, keepdims=False)
    back_pass = jnp.einsum(
        "iy,kyx->kix", window, col_mats, preferred_element_type=jnp.float32
    ).astype(jnp.bfloat16)
    return jnp.einsum(
        "kji,kjx->ix", row_mats, back_pass, preferred_element_type=jnp.float32
    ).astype(jnp.bfloat16)


def apply_all(function, images, models, row_ops, col_ops):
    bound = partial(function, row_ops=row_ops, col_ops=col_ops)
    return lax.map(bound, (images, models.astype(jnp.int32)), batch_size=32)


def per_device(stamps, tile_of, row_offset, col_offset, psf_model, psf_rows, psf_cols, cotangent):
    peer_count = lax.axis_size("tile")
    stamp_count, stamp_rows, stamp_cols = stamps.shape
    block_rows = stamp_rows // 2
    tile_rows, tile_cols = cotangent.shape
    row_blocks = tile_rows // block_rows
    col_blocks = tile_cols // stamp_cols
    capacity = max(2, (5 * stamp_count + 4 * peer_count - 1) // (4 * peer_count))
    slot_total = peer_count * capacity
    row_ops = build_ops(psf_rows, stamp_rows)
    col_ops = build_ops(psf_cols, stamp_cols)
    target = tile_of[:, 0]
    order = jnp.arange(stamp_count, dtype=jnp.int32)
    earlier = (target[None, :] == target[:, None]) & (order[None, :] < order[:, None])
    slots = target * capacity + jnp.sum(earlier.astype(jnp.int32), axis=1)
    slot_ids = jnp.arange(slot_total, dtype=jnp.int32)
    matches = slots[None, :] == slot_ids[:, None]
    place = matches.astype(jnp.bfloat16)
    details = jnp.stack([jnp.ones_like(target), row_offset, col_offset, psf_model], axis=1)
    detail_send = jnp.sum(jnp.where(matches[:, :, None], details[None, :, :], 0), axis=1)
    detail_send = detail_send.reshape(peer_count, capacity, 4)
    raw_send = jnp.dot(
        place,
        stamps.reshape((stamp_count, stamp_rows * stamp_cols)),
        preferred_element_type=jnp.float32,
    )
    raw_send = raw_send.astype(jnp.bfloat16).reshape(peer_count, capacity, stamp_rows, stamp_cols)
    raw_part = lax.all_to_all(raw_send, "tile", split_axis=0, concat_axis=0, tiled=True)
    info_part = lax.all_to_all(detail_send, "tile", split_axis=0, concat_axis=0, tiled=True)
    flat = raw_part.reshape((-1, stamp_rows, stamp_cols))
    result = apply_all(convolve_one, flat, info_part.reshape((-1, 4))[:, 3], row_ops, col_ops)
    received = result.reshape(raw_part.shape)
    info_flat = info_part.reshape((slot_total, 4))
    upper_block = info_flat[:, 1]
    block_ids = jnp.stack([upper_block, upper_block + 1], axis=1) * col_blocks + info_flat[:, 2:3]
    targets = jnp.arange((row_blocks + 1) * col_blocks, dtype=jnp.int32)
    placing = (block_ids.reshape(-1)[None, :] == targets[:, None]).astype(jnp.bfloat16)
    pieces = received.reshape((slot_total * 2, block_rows * stamp_cols))
    extended = jnp.dot(placing, pieces, preferred_element_type=jnp.float32)
    extended = extended.reshape(row_blocks + 1, col_blocks, block_rows, stamp_cols).transpose(
        0, 2, 1, 3
    )
    extended = extended.reshape((row_blocks + 1) * block_rows, tile_cols)
    arriving = passed_along(extended[tile_rows:].astype(jnp.bfloat16), "tile", 1).astype(
        jnp.float32
    )
    tile_sum = extended[:tile_rows].at[:block_rows].add(arriving)
    tile_image = tile_sum.astype(jnp.bfloat16)
    rim = passed_along(cotangent[:block_rows], "tile", -1)
    padded = jnp.concatenate([cotangent, rim], axis=0)
    blocks = padded.reshape(row_blocks + 1, block_rows, col_blocks, stamp_cols).transpose(
        0, 2, 1, 3
    )
    blocks = blocks.reshape((row_blocks + 1) * col_blocks, block_rows * stamp_cols)
    windows = lax.dot_general(
        placing, blocks, (((0,), (0,)), ((), ())), preferred_element_type=jnp.float32
    )
    windows = windows.astype(jnp.bfloat16).reshape(slot_total, stamp_rows, stamp_cols)
    slot_grads = apply_all(transpose_one, windows, info_flat[:, 3], row_ops, col_ops)
    slot_grads = slot_grads.reshape(peer_count, capacity, stamp_rows, stamp_cols)
    returned = lax.all_to_all(
        for_sending(slot_grads), "tile", split_axis=0, concat_axis=0, tiled=True
    ).astype(slot_grads.dtype)
    stamp_grad = lax.dot_general(
        place,
        returned.reshape((slot_total, stamp_rows * stamp_cols)),
        (((0,), (0,)), ((), ())),
        preferred_element_type=jnp.float32,
    )
    stamp_grad = stamp_grad.astype(jnp.bfloat16).reshape(stamp_count, stamp_rows, stamp_cols)
    return (tile_image, stamp_grad)


def solution(mesh):
    in_specs = (
        P(("band", "tile"), None, None),
        P(("band", "tile"), None),
        P(("band", "tile")),
        P(("band", "tile")),
        P(("band", "tile")),
        P("band", None, None),
        P("band", None, None),
        P(("band", "tile"), None),
    )
    out_specs = (P(("band", "tile"), None), P(("band", "tile"), None, None))
    return jax.shard_map(
        per_device, mesh=mesh, in_specs=in_specs, out_specs=out_specs, check_vma=False
    )
```

profile of v0, /device:TPU:0, one launch (start us, length us, event | category | flops | bytes accessed | tf_op | source)
XLA Modules:
  0.0 206.2 jit_solution(8025420480745174259)
XLA Ops:
  3.9 7.4 %all-to-all-start = ((s32[16,10,4]{1,2,0:T(4,128)}), s32[16,10,4]{1,2,0:T(4,128)S(1)}, u32[]{:S(2)}, u32[]{:S(2)}) async-start(s32[16,10,4]{1,2,0:T(4,128)} %copy.35), calls=%async_computation | async-start | bytes 65536 | tf_op jit(solution)/shard_map/all_to_all | solution.py:100
  11.3 3.3 %fusion.40 = bf16[20,8,64,128]{3,1,2,0:T(8,128)(2,1)S(1)} fusion(bf16[16,8,64,128]{3,2,1,0:T(8,128)(2,1)} %bitcast.195, s32[128]{0:T(128)S(1)} %multiply_add_fusion.1), kind=kOutput, calls=%fused_computation.44 | convolution fusion | flops 336875520 | bytes 4719104 | tf_op jit(solution)/shard_map/dot_general | solution.py:93
  14.6 2.2 %copy.53 = bf16[20,8,64,128]{3,2,1,0:T(8,128)(2,1)} copy(bf16[20,8,64,128]{3,1,2,0:T(8,128)(2,1)S(1)} %fusion.40) | data formatting | bytes 5242880
  18.0 5.1 %all-to-all-start.1 = ((bf16[16,10,64,128]{3,2,1,0:T(8,128)(2,1)}), bf16[16,10,64,128]{3,2,1,0:T(8,128)(2,1)}, u32[]{:S(2)}, u32[]{:S(2)}) async-start(bf16[16,10,64,128]{3,2,1,0:T(8,128)(2,1)} %bitcast.45), calls=%async_computation.1 | async-start | bytes 5242880 | tf_op jit(solution)/shard_map/all_to_all | solution.py:99
  29.9 2.4 %convolution_convert_fusion.5 = bf16[320,4096]{1,0:T(8,128)(2,1)} fusion(bf16[36,4096]{1,0:T(8,128)(2,1)S(1)} %bitcast.197, s32[320]{0:T(512)S(1)} %add.114), kind=kOutput, calls=%fused_computation.34 | convolution fusion | flops 95694080 | bytes 2917632 | tf_op jit(solution)/shard_map/dot_general | solution.py:126
  32.3 5.3 %reshape_reshape.10 = bf16[5,32,64,128]{3,2,1,0:T(8,128)(2,1)} reshape(bf16[320,4096]{1,0:T(8,128)(2,1)} %convolution_convert_fusion.5) | data formatting | bytes 5242880 | tf_op jit(solution)/shard_map/reshape;reshape | solution.py:69
  39.9 45.1 %while.22 = (s32[]{:T(128)}, bf16[5,32,64,128]{3,2,1,0:T(8,128)(2,1)}, s32[5,32]{1,0:T(8,128)S(1)}, bf16[18,3,64,64]{3,2,1,0:T(8,128)(2,1)S(1)}, bf16[18,3,128,1...) while((s32[]{:T(128)}, bf16[5,32,64,128]{3,2,1,0:T(8,128)(2,1)}, ...), condition=%wide.region_5.6_spmd, body=%wide.region_4.5_spmd.sunk | while | flops 303038624 | bytes 13633873 | solution.py:69
  39.9 2.6 %gather_fusion.3 = bf16[32,3,128,128]{3,2,1,0:T(8,128)(2,1)} fusion(bf16[18,3,128,128]{3,2,1,0:T(8,128)(2,1)S(1)} %get-tuple-element.221, s32[32]{0:T(128)S(1)} %shift-left_bitcast_fusion.5), kind=kCustom, calls=%fused_computation.3.clone.1 | custom fusion | bytes 6291968 | tf_op jit(solution)/shard_map/while/body/eval_jaxpr/vmap(jit(dynamic_index_in_dim))/gather | solution.py:58
  44.4 4.5 %fusion.85 = bf16[5,32,64,128]{3,2,1,0:T(8,128)(2,1)} fusion(bf16[5,32,64,128]{3,2,1,0:T(8,128)(2,1)} %get-tuple-element.211, s32[]{:T(128)} %get-tuple-element.210, bf16[32,3,64,64]{3,2,1,0:T(8,128)(2,1)} %gather_fusion.2, bf16[32,3,128,128]{3,2,1,0:T(8,128)(2,1)} %gather_fusion.3, bf16[5,32,64,128]{3,2,1,0:T(8,128)(2,1)} %get-tuple-element.222), kind=kOutput, calls=%fused_computation.23.clone.1 | convolution fusion | flops 303038464 | bytes 5768192 | tf_op jit(solution)/shard_map/while/body/eval_jaxpr/vmap(kji,kjx->ix)/dot_general | solution.py:62
  48.9 2.6 %gather_fusion.3 = bf16[32,3,128,128]{3,2,1,0:T(8,128)(2,1)} fusion(bf16[18,3,128,128]{3,2,1,0:T(8,128)(2,1)S(1)} %get-tuple-element.221, s32[32]{0:T(128)S(1)} %shift-left_bitcast_fusion.5), kind=kCustom, calls=%fused_computation.3.clone.1 | custom fusion | bytes 6291968 | tf_op jit(solution)/shard_map/while/body/eval_jaxpr/vmap(jit(dynamic_index_in_dim))/gather | solution.py:58
  53.4 4.5 %fusion.85 = bf16[5,32,64,128]{3,2,1,0:T(8,128)(2,1)} fusion(bf16[5,32,64,128]{3,2,1,0:T(8,128)(2,1)} %get-tuple-element.211, s32[]{:T(128)} %get-tuple-element.210, bf16[32,3,64,64]{3,2,1,0:T(8,128)(2,1)} %gather_fusion.2, bf16[32,3,128,128]{3,2,1,0:T(8,128)(2,1)} %gather_fusion.3, bf16[5,32,64,128]{3,2,1,0:T(8,128)(2,1)} %get-tuple-element.222), kind=kOutput, calls=%fused_computation.23.clone.1 | convolution fusion | flops 303038464 | bytes 5768192 | tf_op jit(solution)/shard_map/while/body/eval_jaxpr/vmap(kji,kjx->ix)/dot_general | solution.py:62
  57.9 2.6 %gather_fusion.3 = bf16[32,3,128,128]{3,2,1,0:T(8,128)(2,1)} fusion(bf16[18,3,128,128]{3,2,1,0:T(8,128)(2,1)S(1)} %get-tuple-element.221, s32[32]{0:T(128)S(1)} %shift-left_bitcast_fusion.5), kind=kCustom, calls=%fused_computation.3.clone.1 | custom fusion | bytes 6291968 | tf_op jit(solution)/shard_map/while/body/eval_jaxpr/vmap(jit(dynamic_index_in_dim))/gather | solution.py:58
  62.4 4.5 %fusion.85 = bf16[5,32,64,128]{3,2,1,0:T(8,128)(2,1)} fusion(bf16[5,32,64,128]{3,2,1,0:T(8,128)(2,1)} %get-tuple-element.211, s32[]{:T(128)} %get-tuple-element.210, bf16[32,3,64,64]{3,2,1,0:T(8,128)(2,1)} %gather_fusion.2, bf16[32,3,128,128]{3,2,1,0:T(8,128)(2,1)} %gather_fusion.3, bf16[5,32,64,128]{3,2,1,0:T(8,128)(2,1)} %get-tuple-element.222), kind=kOutput, calls=%fused_computation.23.clone.1 | convolution fusion | flops 303038464 | bytes 5768192 | tf_op jit(solution)/shard_map/while/body/eval_jaxpr/vmap(kji,kjx->ix)/dot_general | solution.py:62
  66.9 2.6 %gather_fusion.3 = bf16[32,3,128,128]{3,2,1,0:T(8,128)(2,1)} fusion(bf16[18,3,128,128]{3,2,1,0:T(8,128)(2,1)S(1)} %get-tuple-element.221, s32[32]{0:T(128)S(1)} %shift-left_bitcast_fusion.5), kind=kCustom, calls=%fused_computation.3.clone.1 | custom fusion | bytes 6291968 | tf_op jit(solution)/shard_map/while/body/eval_jaxpr/vmap(jit(dynamic_index_in_dim))/gather | solution.py:58
  71.4 4.5 %fusion.85 = bf16[5,32,64,128]{3,2,1,0:T(8,128)(2,1)} fusion(bf16[5,32,64,128]{3,2,1,0:T(8,128)(2,1)} %get-tuple-element.211, s32[]{:T(128)} %get-tuple-element.210, bf16[32,3,64,64]{3,2,1,0:T(8,128)(2,1)} %gather_fusion.2, bf16[32,3,128,128]{3,2,1,0:T(8,128)(2,1)} %gather_fusion.3, bf16[5,32,64,128]{3,2,1,0:T(8,128)(2,1)} %get-tuple-element.222), kind=kOutput, calls=%fused_computation.23.clone.1 | convolution fusion | flops 303038464 | bytes 5768192 | tf_op jit(solution)/shard_map/while/body/eval_jaxpr/vmap(kji,kjx->ix)/dot_general | solution.py:62
  75.9 2.6 %gather_fusion.3 = bf16[32,3,128,128]{3,2,1,0:T(8,128)(2,1)} fusion(bf16[18,3,128,128]{3,2,1,0:T(8,128)(2,1)S(1)} %get-tuple-element.221, s32[32]{0:T(128)S(1)} %shift-left_bitcast_fusion.5), kind=kCustom, calls=%fused_computation.3.clone.1 | custom fusion | bytes 6291968 | tf_op jit(solution)/shard_map/while/body/eval_jaxpr/vmap(jit(dynamic_index_in_dim))/gather | solution.py:58
  80.4 4.5 %fusion.85 = bf16[5,32,64,128]{3,2,1,0:T(8,128)(2,1)} fusion(bf16[5,32,64,128]{3,2,1,0:T(8,128)(2,1)} %get-tuple-element.211, s32[]{:T(128)} %get-tuple-element.210, bf16[32,3,64,64]{3,2,1,0:T(8,128)(2,1)} %gather_fusion.2, bf16[32,3,128,128]{3,2,1,0:T(8,128)(2,1)} %gather_fusion.3, bf16[5,32,64,128]{3,2,1,0:T(8,128)(2,1)} %get-tuple-element.222), kind=kOutput, calls=%fused_computation.23.clone.1 | convolution fusion | flops 303038464 | bytes 5768192 | tf_op jit(solution)/shard_map/while/body/eval_jaxpr/vmap(kji,kjx->ix)/dot_general | solution.py:62
  85.0 56.5 %all-to-all-start.2 = ((bf16[16,10,64,128]{3,2,1,0:T(8,128)(2,1)}), bf16[16,10,64,128]{3,2,1,0:T(8,128)(2,1)}, u32[]{:S(2)}, u32[]{:S(2)}) async-start(bf16[16,10,64,128]{3,2,1,0:T(8,128)(2,1)} %bitcast.192), calls=%async_computation.2 | async-start | bytes 5242880 | tf_op jit(solution)/shard_map/all_to_all | solution.py:132
  143.7 48.9 %while.21 = (s32[]{:T(128)}, bf16[5,32,64,128]{3,2,1,0:T(8,128)(2,1)}, s32[5,32]{1,0:T(8,128)S(1)}, bf16[18,3,64,64]{3,2,1,0:T(8,128)(2,1)S(1)}, bf16[5,32,64,12...) while((s32[]{:T(128)}, bf16[5,32,64,128]{3,2,1,0:T(8,128)(2,1)}, ...), condition=%wide.region_3.4_spmd, body=%wide.region_2.3_spmd.sunk | while | flops 303038624 | bytes 13633873 | solution.py:69
  143.7 2.6 %gather_fusion = bf16[32,3,128,128]{3,2,1,0:T(8,128)(2,1)} fusion(bf16[18,3,128,128]{3,2,1,0:T(8,128)(2,1)S(1)} %get-tuple-element.201, s32[32]{0:T(128)S(1)} %shift-left_bitcast_fusion.4), kind=kCustom, calls=%fused_computation.1.clone.1 | custom fusion | bytes 6291968 | tf_op jit(solution)/shard_map/while/body/eval_jaxpr/vmap(jit(dynamic_index_in_dim))/gather | solution.py:46
  148.2 5.3 %fusion.80 = bf16[5,32,64,128]{3,2,1,0:T(8,128)(2,1)} fusion(bf16[5,32,64,128]{3,2,1,0:T(8,128)(2,1)} %get-tuple-element.190, s32[]{:T(128)} %get-tuple-element.189, bf16[32,3,128,128]{3,2,1,0:T(8,128)(2,1)} %gather_fusion, bf16[32,3,64,64]{3,2,1,0:T(8,128)(2,1)} %gather_fusion.1, bf16[5,32,64,128]{3,2,1,0:T(8,128)(2,1)} %get-tuple-element.200), kind=kOutput, calls=%fused_computation.9.clone.1 | convolution fusion | flops 303038464 | bytes 5768192 | tf_op jit(solution)/shard_map/while/body/eval_jaxpr/vmap(kix,kyx->iy)/dot_general | solution.py:50
  153.5 2.6 %gather_fusion = bf16[32,3,128,128]{3,2,1,0:T(8,128)(2,1)} fusion(bf16[18,3,128,128]{3,2,1,0:T(8,128)(2,1)S(1)} %get-tuple-element.201, s32[32]{0:T(128)S(1)} %shift-left_bitcast_fusion.4), kind=kCustom, calls=%fused_computation.1.clone.1 | custom fusion | bytes 6291968 | tf_op jit(solution)/shard_map/while/body/eval_jaxpr/vmap(jit(dynamic_index_in_dim))/gather | solution.py:46
  158.0 5.3 %fusion.80 = bf16[5,32,64,128]{3,2,1,0:T(8,128)(2,1)} fusion(bf16[5,32,64,128]{3,2,1,0:T(8,128)(2,1)} %get-tuple-element.190, s32[]{:T(128)} %get-tuple-element.189, bf16[32,3,128,128]{3,2,1,0:T(8,128)(2,1)} %gather_fusion, bf16[32,3,64,64]{3,2,1,0:T(8,128)(2,1)} %gather_fusion.1, bf16[5,32,64,128]{3,2,1,0:T(8,128)(2,1)} %get-tuple-element.200), kind=kOutput, calls=%fused_computation.9.clone.1 | convolution fusion | flops 303038464 | bytes 5768192 | tf_op jit(solution)/shard_map/while/body/eval_jaxpr/vmap(kix,kyx->iy)/dot_general | solution.py:50
  163.3 2.6 %gather_fusion = bf16[32,3,128,128]{3,2,1,0:T(8,128)(2,1)} fusion(bf16[18,3,128,128]{3,2,1,0:T(8,128)(2,1)S(1)} %get-tuple-element.201, s32[32]{0:T(128)S(1)} %shift-left_bitcast_fusion.4), kind=kCustom, calls=%fused_computation.1.clone.1 | custom fusion | bytes 6291968 | tf_op jit(solution)/shard_map/while/body/eval_jaxpr/vmap(jit(dynamic_index_in_dim))/gather | solution.py:46
  167.8 5.2 %fusion.80 = bf16[5,32,64,128]{3,2,1,0:T(8,128)(2,1)} fusion(bf16[5,32,64,128]{3,2,1,0:T(8,128)(2,1)} %get-tuple-element.190, s32[]{:T(128)} %get-tuple-element.189, bf16[32,3,128,128]{3,2,1,0:T(8,128)(2,1)} %gather_fusion, bf16[32,3,64,64]{3,2,1,0:T(8,128)(2,1)} %gather_fusion.1, bf16[5,32,64,128]{3,2,1,0:T(8,128)(2,1)} %get-tuple-element.200), kind=kOutput, calls=%fused_computation.9.clone.1 | convolution fusion | flops 303038464 | bytes 5768192 | tf_op jit(solution)/shard_map/while/body/eval_jaxpr/vmap(kix,kyx->iy)/dot_general | solution.py:50
  173.1 2.6 %gather_fusion = bf16[32,3,128,128]{3,2,1,0:T(8,128)(2,1)} fusion(bf16[18,3,128,128]{3,2,1,0:T(8,128)(2,1)S(1)} %get-tuple-element.201, s32[32]{0:T(128)S(1)} %shift-left_bitcast_fusion.4), kind=kCustom, calls=%fused_computation.1.clone.1 | custom fusion | bytes 6291968 | tf_op jit(solution)/shard_map/while/body/eval_jaxpr/vmap(jit(dynamic_index_in_dim))/gather | solution.py:46
  177.6 5.2 %fusion.80 = bf16[5,32,64,128]{3,2,1,0:T(8,128)(2,1)} fusion(bf16[5,32,64,128]{3,2,1,0:T(8,128)(2,1)} %get-tuple-element.190, s32[]{:T(128)} %get-tuple-element.189, bf16[32,3,128,128]{3,2,1,0:T(8,128)(2,1)} %gather_fusion, bf16[32,3,64,64]{3,2,1,0:T(8,128)(2,1)} %gather_fusion.1, bf16[5,32,64,128]{3,2,1,0:T(8,128)(2,1)} %get-tuple-element.200), kind=kOutput, calls=%fused_computation.9.clone.1 | convolution fusion | flops 303038464 | bytes 5768192 | tf_op jit(solution)/shard_map/while/body/eval_jaxpr/vmap(kix,kyx->iy)/dot_general | solution.py:50
  182.8 2.6 %gather_fusion = bf16[32,3,128,128]{3,2,1,0:T(8,128)(2,1)} fusion(bf16[18,3,128,128]{3,2,1,0:T(8,128)(2,1)S(1)} %get-tuple-element.201, s32[32]{0:T(128)S(1)} %shift-left_bitcast_fusion.4), kind=kCustom, calls=%fused_computation.1.clone.1 | custom fusion | bytes 6291968 | tf_op jit(solution)/shard_map/while/body/eval_jaxpr/vmap(jit(dynamic_index_in_dim))/gather | solution.py:46
  187.3 5.3 %fusion.80 = bf16[5,32,64,128]{3,2,1,0:T(8,128)(2,1)} fusion(bf16[5,32,64,128]{3,2,1,0:T(8,128)(2,1)} %get-tuple-element.190, s32[]{:T(128)} %get-tuple-element.189, bf16[32,3,128,128]{3,2,1,0:T(8,128)(2,1)} %gather_fusion, bf16[32,3,64,64]{3,2,1,0:T(8,128)(2,1)} %gather_fusion.1, bf16[5,32,64,128]{3,2,1,0:T(8,128)(2,1)} %get-tuple-element.200), kind=kOutput, calls=%fused_computation.9.clone.1 | convolution fusion | flops 303038464 | bytes 5768192 | tf_op jit(solution)/shard_map/while/body/eval_jaxpr/vmap(kix,kyx->iy)/dot_general | solution.py:50
  192.6 3.8 %reshape_reshape_reshape.3 = bf16[320,4096]{1,0:T(8,128)(2,1)S(1)} reshape(bf16[5,32,64,128]{3,2,1,0:T(8,128)(2,1)} %get-tuple-element.78) | data formatting | bytes 5242880 | tf_op jit(solution)/shard_map/reshape;reshape;reshape | solution.py:109
  197.6 2.3 %collective-permute-start = (bf16[32,512]{1,0:T(8,128)(2,1)S(1)}, bf16[32,512]{1,0:T(8,128)(2,1)S(1)}, u32[]{:S(2)}, u32[]{:S(2)}) collective-permute-start(bf16[32,512]{1,0:T(8,128)(2,1)S(1)} %bitcast.204), channel_id=1, source_target_pairs={{0,2},{2,4},{4,6},{6,8},{8,10},{10,12},{12,14},{14,16},{16,18},{18... | collective-permute-start | bytes 98312 | tf_op jit(solution)/shard_map/ppermute | solution.py:12
  199.9 3.7 %fusion.43 = bf16[16,8,64,128]{3,1,2,0:T(8,128)(2,1)S(1)} fusion(bf16[20,8,64,128]{3,2,1,0:T(8,128)(2,1)} %bitcast.65, s32[128]{0:T(128)S(1)} %multiply_add_fusion.1), kind=kOutput, calls=%fused_computation.45 | convolution fusion | flops 336613376 | bytes 4719104 | tf_op jit(solution)/shard_map/dot_general | solution.py:135
  (81 shorter events, 38.3 us)
Async XLA Ops:
  3.9 14.0 %all-to-all-start = ((s32[16,10,4]{1,2,0:T(4,128)}), s32[16,10,4]{1,2,0:T(4,128)S(1)}, u32[]{:S(2)}, u32[]{:S(2)}) async-start(s32[16,10,4]{1,2,0:T(4,128)} %copy.35), calls=%async_computation | async-start | bytes 65536 | tf_op jit(solution)/shard_map/all_to_all | solution.py:100
  18.0 5.1 %copy-start = (bf16[256,512]{1,0:T(8,128)(2,1)S(1)}, bf16[256,512]{1,0:T(8,128)(2,1)}, u32[]{:S(2)}) copy-start(bf16[256,512]{1,0:T(8,128)(2,1)} %param.21) | copy-start | bytes 786436
  18.0 6.4 %copy-start.2 = (f32[18,3,15]{0,2,1:T(8,128)S(1)}, f32[18,3,15]{0,2,1:T(8,128)}, u32[]{:S(2)}) copy-start(f32[18,3,15]{0,2,1:T(8,128)} %param.20) | copy-start | bytes 9724
  18.0 67.0 %all-to-all-start.1 = ((bf16[16,10,64,128]{3,2,1,0:T(8,128)(2,1)}), bf16[16,10,64,128]{3,2,1,0:T(8,128)(2,1)}, u32[]{:S(2)}, u32[]{:S(2)}) async-start(bf16[16,10,64,128]{3,2,1,0:T(8,128)(2,1)} %bitcast.45), calls=%async_computation.1 | async-start | bytes 5242880 | tf_op jit(solution)/shard_map/all_to_all | solution.py:99
  23.1 6.5 %collective-permute-start.1 = (bf16[32,512]{1,0:T(8,128)(2,1)S(1)}, bf16[32,512]{1,0:T(8,128)(2,1)S(1)}, u32[]{:S(2)}, u32[]{:S(2)}) collective-permute-start(bf16[32,512]{1,0:T(8,128)(2,1)S(1)} %slice.52), channel_id=1, source_target_pairs={{2,0},{4,2},{6,4},{8,6},{10,8},{12,10},{14,12},{16,14},{18,16},{20... | collective-permute-start | bytes 98312 | tf_op jit(solution)/shard_map/ppermute | solution.py:12
  26.7 0.7 copy-start.3
  85.0 115.0 %all-to-all-start.2 = ((bf16[16,10,64,128]{3,2,1,0:T(8,128)(2,1)}), bf16[16,10,64,128]{3,2,1,0:T(8,128)(2,1)}, u32[]{:S(2)}, u32[]{:S(2)}) async-start(bf16[16,10,64,128]{3,2,1,0:T(8,128)(2,1)} %bitcast.192), calls=%async_computation.2 | async-start | bytes 5242880 | tf_op jit(solution)/shard_map/all_to_all | solution.py:132
  197.6 7.9 %collective-permute-start = (bf16[32,512]{1,0:T(8,128)(2,1)S(1)}, bf16[32,512]{1,0:T(8,128)(2,1)S(1)}, u32[]{:S(2)}, u32[]{:S(2)}) collective-permute-start(bf16[32,512]{1,0:T(8,128)(2,1)S(1)} %bitcast.204), channel_id=1, source_target_pairs={{0,2},{2,4},{4,6},{6,8},{8,10},{10,12},{12,14},{14,16},{16,18},{18... | collective-permute-start | bytes 98312 | tf_op jit(solution)/shard_map/ppermute | solution.py:12
  205.5 0.7 copy-start.1
where the time goes:
time: 208 us; the launch traced here: 206 us
  starting transfers between devices  72.5 us (35%)
  local copies, waits for them, and re-layouts  67.9 us (33%)
  matrix products  61 us (29%)
  other arithmetic  2.75 us (1%)
    all_to_all x1, starting transfers between devices, per_device(): lax.all_to_all(for_sending(slot_grads), 'tile', split_axis=0, concat_axis...  56.5 us
    dot_general x5, matrix products, convolve_one(): jnp.einsum('kix,kyx->iy', row_pass, col_mats, preferred_element_type=jnp....  26.3 us
    dot_general x5, matrix products, transpose_one(): jnp.einsum('kji,kjx->ix', row_mats, back_pass, preferred_element_type=jnp...  22.5 us
    gather x5, local copies, waits for them, and re-layouts, convolve_one(): col_mats = lax.dynamic_index_in_dim(col_ops, model, 0, keepdims=False)  13 us
    gather x5, local copies, waits for them, and re-layouts, transpose_one(): col_mats = lax.dynamic_index_in_dim(col_ops, model, 0, keepdims=False)  13 us
    gather x5, local copies, waits for them, and re-layouts, convolve_one(): row_mats = lax.dynamic_index_in_dim(row_ops, model, 0, keepdims=False)  9.5 us
    gather x5, local copies, waits for them, and re-layouts, transpose_one(): row_mats = lax.dynamic_index_in_dim(row_ops, model, 0, keepdims=False)  9.5 us
    all_to_all x1, starting transfers between devices, per_device(): lax.all_to_all(detail_send, 'tile', split_axis=0, concat_axis=0, tiled=True)  7.39 us
  transfers between devices with their start and end apart: 5, of which 1 were waited for; matrix products, arithmetic and copies ran while one was open for 62% of the time, Pallas kernels for 0%

commit v1 on v0

--- a/solution.py
+++ b/solution.py
@@ -3,6 +3,8 @@
 import jax
 import jax.numpy as jnp
 from jax import lax
+from jax.experimental import pallas as pl
+from jax.experimental.pallas import tpu as pltpu
 from jax.sharding import PartitionSpec as P
 
 
@@ -142,6 +144,212 @@
     return (tile_image, stamp_grad)
 
 
+def tap_rows(profiles, lanes, flip):
+    models, terms, count = profiles.shape
+    half = (count - 1) // 2
+    flat = profiles.reshape((models * terms, count))
+    if flip:
+        flat = flat[:, ::-1]
+    gap = jnp.zeros((models * terms, lanes - count), flat.dtype)
+    return jnp.concatenate([flat[:, half:], gap, flat[:, :half]], axis=1)
+
+
+def band_matrix(row, size, half):
+    lanes = row.shape[-1]
+    spread = jnp.broadcast_to(row, (size, lanes))
+    turned = pltpu.roll(spread, 0, 1, stride=1, stride_axis=0)
+    down = lax.broadcasted_iota(jnp.int32, (size, lanes), 0)
+    across = lax.broadcasted_iota(jnp.int32, (size, lanes), 1)
+    return jnp.where(jnp.abs(across - down) <= half, turned, 0.0).astype(jnp.bfloat16)
+
+
+def forward_kernel(half, terms, model_bits, col_blocks, group, codes, rows_ref, cols_ref, stamps_ref,
+                   strip_ref, row_ops, col_ops, total):
+    step = pl.program_id(0)
+    models, stacked, stamp_rows = row_ops.shape
+    stamp_cols = col_ops.shape[2]
+    block_rows = stamp_rows // 2
+    strip_rows = strip_ref.shape[0]
+
+    @pl.when(step == 0)
+    def _():
+        def build(m, carry):
+            for k in range(terms):
+                line = m * terms + k
+                mat = band_matrix(rows_ref[pl.ds(line, 1), :], stamp_rows, half)
+                row_ops[m, k * stamp_rows:(k + 1) * stamp_rows, :] = mat[:, :stamp_rows]
+                col_ops[m, k * stamp_cols:(k + 1) * stamp_cols, :] = band_matrix(
+                    cols_ref[pl.ds(line, 1), :], stamp_cols, half)
+            return carry
+
+        lax.fori_loop(0, models, build, 0)
+
+        def clear(i, carry):
+            total[pl.ds(pl.multiple_of(i * block_rows, block_rows), block_rows), :] = jnp.zeros(
+                (block_rows, total.shape[1]), jnp.float32)
+            return carry
+
+        lax.fori_loop(0, total.shape[0] // block_rows, clear, 0)
+
+    per_step = stamps_ref.shape[0]
+
+    def some(g, carry):
+        done = []
+        for u in range(group):
+            local = g * group + u
+            code = codes[step * per_step + local]
+            model = code & ((1 << model_bits) - 1)
+            block = code >> model_bits
+            first = jnp.dot(row_ops[model], stamps_ref[local],
+                            preferred_element_type=jnp.float32).astype(jnp.bfloat16)
+            wide = jnp.concatenate(
+                [first[k * stamp_rows:(k + 1) * stamp_rows] for k in range(terms)], axis=1)
+            out = jnp.dot(wide, col_ops[model], preferred_element_type=jnp.float32)
+            done.append((block, out.astype(jnp.bfloat16).astype(jnp.float32)))
+        for block, out in done:
+            top = pl.multiple_of((block // col_blocks) * block_rows, block_rows)
+            left = pl.multiple_of((block % col_blocks) * stamp_cols, stamp_cols)
+            spot = (pl.ds(top, stamp_rows), pl.ds(left, stamp_cols))
+            total[spot] = total[spot] + out
+        return carry
+
+    lax.fori_loop(0, per_step // group, some, 0)
+
+    @pl.when(step == pl.num_programs(0) - 1)
+    def _():
+        def put(i, carry):
+            spot = pl.ds(pl.multiple_of(i * block_rows, block_rows), block_rows)
+            strip_ref[spot, :] = total[spot, :].astype(jnp.bfloat16)
+            return carry
+
+        lax.fori_loop(0, strip_rows // block_rows, put, 0)
+
+
+def backward_kernel(half, terms, model_bits, col_blocks, group, codes, rows_ref, cols_ref, sky_ref,
+                    grads_ref, row_ops, col_ops, sky, sem):
+    step = pl.program_id(0)
+    models, stamp_rows, stacked = row_ops.shape
+    stamp_cols = col_ops.shape[1]
+    block_rows = stamp_rows // 2
+    strip_rows = sky_ref.shape[0]
+
+    @pl.when(step == 0)
+    def _():
+        copy = pltpu.make_async_copy(sky_ref, sky.at[pl.ds(0, strip_rows)], sem)
+        copy.start()
+
+        def build(m, carry):
+            mats = []
+            for k in range(terms):
+                line = m * terms + k
+                mat = band_matrix(rows_ref[pl.ds(line, 1), :], stamp_rows, half)
+                mats.append(mat[:, :stamp_rows])
+                col_ops[m, :, k * stamp_cols:(k + 1) * stamp_cols] = band_matrix(
+                    cols_ref[pl.ds(line, 1), :], stamp_cols, half)
+            row_ops[m] = jnp.concatenate(mats, axis=1)
+            return carry
+
+        lax.fori_loop(0, models, build, 0)
+        sky[strip_rows:, :] = jnp.zeros((block_rows, sky.shape[1]), jnp.bfloat16)
+        copy.wait()
+
+    per_step = grads_ref.shape[0]
+
+    def some(g, carry):
+        done = []
+        for u in range(group):
+            local = g * group + u
+            code = codes[step * per_step + local]
+            model = code & ((1 << model_bits) - 1)
+            block = code >> model_bits
+            top = pl.multiple_of((block // col_blocks) * block_rows, block_rows)
+            left = pl.multiple_of((block % col_blocks) * stamp_cols, stamp_cols)
+            window = sky[pl.ds(top, stamp_rows), pl.ds(left, stamp_cols)]
+            first = jnp.dot(window, col_ops[model],
+                            preferred_element_type=jnp.float32).astype(jnp.bfloat16)
+            tall = jnp.concatenate(
+                [first[:, k * stamp_cols:(k + 1) * stamp_cols] for k in range(terms)], axis=0)
+            out = jnp.dot(row_ops[model], tall, preferred_element_type=jnp.float32)
+            done.append(out.astype(jnp.bfloat16))
+        for u in range(group):
+            grads_ref[g * group + u] = done[u]
+        return carry
+
+    lax.fori_loop(0, per_step // group, some, 0)
+
+
+def divisor(number, wanted):
+    return max(d for d in range(1, wanted + 1) if number % d == 0)
+
+
+def in_place(stamps, tile_of, row_offset, col_offset, psf_model, psf_rows, psf_cols, cotangent):
+    peers = lax.axis_size("tile")
+    stamp_count, stamp_rows, stamp_cols = stamps.shape
+    models, terms, taps = psf_rows.shape
+    half = (taps - 1) // 2
+    block_rows = stamp_rows // 2
+    tile_rows, tile_cols = cotangent.shape
+    row_blocks = tile_rows // block_rows
+    col_blocks = tile_cols // stamp_cols
+    strip_rows = peers * tile_rows
+    model_bits = max(1, (models - 1).bit_length())
+    upper = tile_of[:, 0] * row_blocks + row_offset
+    codes = ((upper * col_blocks + col_offset) << model_bits) + psf_model
+    lanes = 128
+    per_step = divisor(stamp_count, 16)
+    group = divisor(per_step, 8)
+    grid = (stamp_count // per_step,)
+    flops = 2 * stamp_count * terms * stamp_rows * stamp_cols * (stamp_rows + stamp_cols)
+    smem = pl.BlockSpec(memory_space=pltpu.SMEM)
+    table = pl.BlockSpec((models * terms, lanes), lambda i: (0, 0))
+    pieces = pl.BlockSpec((per_step, stamp_rows, stamp_cols), lambda i: (i, 0, 0))
+    params = pltpu.CompilerParams(vmem_limit_bytes=40 << 20)
+
+    sky = lax.all_gather(cotangent, "tile", axis=0, tiled=True)
+    strip = pl.pallas_call(
+        partial(forward_kernel, half, terms, model_bits, col_blocks, group),
+        grid=grid,
+        out_shape=jax.ShapeDtypeStruct((strip_rows, tile_cols), jnp.bfloat16),
+        in_specs=[smem, table, table, pieces],
+        out_specs=pl.BlockSpec((strip_rows, tile_cols), lambda i: (0, 0)),
+        scratch_shapes=[
+            pltpu.VMEM((models, terms * stamp_rows, stamp_rows), jnp.bfloat16),
+            pltpu.VMEM((models, terms * stamp_cols, stamp_cols), jnp.bfloat16),
+            pltpu.VMEM((strip_rows + block_rows, tile_cols), jnp.float32),
+        ],
+        compiler_params=params,
+        cost_estimate=pl.CostEstimate(flops=8 * flops, bytes_accessed=40 << 20, transcendentals=0),
+    )(codes, tap_rows(psf_rows, lanes, False), tap_rows(psf_cols, lanes, True), stamps)
+    tile_image = lax.psum_scatter(strip, "tile", scatter_dimension=0, tiled=True)
+    stamp_grad = pl.pallas_call(
+        partial(backward_kernel, half, terms, model_bits, col_blocks, group),
+        grid=grid,
+        out_shape=jax.ShapeDtypeStruct(stamps.shape, jnp.bfloat16),
+        in_specs=[smem, table, table, pl.BlockSpec(memory_space=pl.ANY)],
+        out_specs=pieces,
+        scratch_shapes=[
+            pltpu.VMEM((models, stamp_rows, terms * stamp_rows), jnp.bfloat16),
+            pltpu.VMEM((models, stamp_cols, terms * stamp_cols), jnp.bfloat16),
+            pltpu.VMEM((strip_rows + block_rows, tile_cols), jnp.bfloat16),
+            pltpu.SemaphoreType.DMA,
+        ],
+        compiler_params=params,
+        cost_estimate=pl.CostEstimate(flops=8 * flops, bytes_accessed=40 << 20, transcendentals=0),
+    )(codes, tap_rows(psf_rows, lanes, True), tap_rows(psf_cols, lanes, False), sky)
+    return tile_image, stamp_grad
+
+
+def strip_fits(peers, cotangent):
+    rows, cols = cotangent.shape
+    return peers * rows * cols * 4 <= 12 << 20
+
+
+def per_device_any(*args):
+    if strip_fits(lax.axis_size("tile"), args[-1]):
+        return in_place(*args)
+    return per_device(*args)
+
+
 def solution(mesh):
     in_specs = (
         P(("band", "tile"), None, None),
@@ -155,5 +363,5 @@
     )
     out_specs = (P(("band", "tile"), None), P(("band", "tile"), None, None))
     return jax.shard_map(
-        per_device, mesh=mesh, in_specs=in_specs, out_specs=out_specs, check_vma=False
-    )
+        per_device_any, mesh=mesh, in_specs=in_specs, out_specs=out_specs, check_vma=False
+    )

time: 208 us -> 146 us (0.70)
  starting transfers between devices: 72.5 us -> 0.08 us
  waiting for transfers between devices: 1.09 us -> 73.4 us
  matrix products: 61 us -> 0 us
  local copies, waits for them, and re-layouts: 67.9 us -> 8.03 us
  Pallas kernels: 0 us -> 49.4 us
  between operations: 0.97 us -> 14.1 us
    all_to_all x3 -> x0, starting transfers between devices: 69 us -> none  [the longest x1 56.5 us: per_device(): lax.all_to_all(for_sending(slot_grads), 'tile', split_axis=0, concat_axis...]
    dot_general x16 -> x0, matrix products: 61 us -> none  [the longest x5 26.3 us: convolve_one(): jnp.einsum('kix,kyx->iy', row_pass, col_mats, preferred_element_type=jnp....]
    reduce_scatter x0 -> x1, waiting for transfers between devices: none -> 49.6 us  [in_place(): lax.psum_scatter(strip, 'tile', scatter_dimension=0, tiled=True)]
    pallas_call x0 -> x2, Pallas kernels: none -> 49.4 us  [the longest x1 25.8 us: in_place(): pl.pallas_call(partial(forward_kernel, half, terms, model_bits, col_block...]
    gather x20 -> x0, local copies, waits for them, and re-layouts: 45 us -> none  [the longest x5 13 us: convolve_one(): col_mats = lax.dynamic_index_in_dim(col_ops, model, 0, keepdims=False)]
    all_gather x0 -> x1, waiting for transfers between devices: none -> 23.1 us  [in_place(): sky = lax.all_gather(cotangent, 'tile', axis=0, tiled=True)]
    another operation x8 -> x1, local copies, waits for them, and re-layouts: 13.8 us -> 0.01 us  [the longest x2 5.37 us: apply_all(): return lax.map(bound, (images, models.astype(jnp.int32)), batch_size=32)]
    ppermute x2 -> x0, starting transfers between devices: 3.55 us -> none  [passed_along(): return lax.ppermute(array, axis, pairs)]
  transfers between devices with their start and end apart: 5 -> 2, of which waited for: 1 -> 2; matrix products, arithmetic and copies ran while one was open for 62% -> 2% of each run, Pallas kernels for 0% -> 34%
where the time goes in v1:
time: 146 us
  waiting for transfers between devices  73.4 us (50%)
  Pallas kernels  49.4 us (34%)
  between operations  14.1 us (10%)
  local copies, waits for them, and re-layouts  8.03 us (5%)
    reduce_scatter x1, waiting for transfers between devices, in_place(): lax.psum_scatter(strip, 'tile', scatter_dimension=0, tiled=True)  49.6 us
    pallas_call x1, Pallas kernels, in_place(): pl.pallas_call(partial(forward_kernel, half, terms, model_bits, col_block...  25.8 us
    pallas_call x1, Pallas kernels, in_place(): pl.pallas_call(partial(backward_kernel, half, terms, model_bits, col_bloc...  23.6 us
    all_gather x1, waiting for transfers between devices, in_place(): sky = lax.all_gather(cotangent, 'tile', axis=0, tiled=True)  23.1 us
    unnamed x8, local copies, waits for them, and re-layouts  7.44 us
  transfers between devices with their start and end apart: 2, of which 2 were waited for; matrix products, arithmetic and copies ran while one was open for 2% of the time, Pallas kernels for 34%

profile of v1, /device:TPU:0, one launch (start us, length us, event | category | flops | bytes accessed | tf_op | source)
XLA Modules:
  0.0 145.8 jit_solution(4149735185146536718)
XLA Ops:
  7.2 0.0 all-gather.2.cloned.1.call-start
  7.2 0.7 all-gather.2.cloned.1.call-update
  7.9 0.0 reduce-scatter.2.cloned.1.call-start
  7.9 0.8 copy.12
  8.8 0.8 copy.13
  9.7 0.1 fusion.3
  9.8 0.1 slice.41
  9.8 0.1 slice.45
  9.9 0.1 fusion.2
  10.0 0.1 slice.39
  10.1 0.1 slice.43
  10.2 0.1 pad.10.clone
  10.2 0.7 shift-left_add_fusion.codes
  11.0 0.1 pad_maximum_fusion.3
  11.1 0.0 copy-start.2
  11.1 1.6 %copy-done.2 = bf16[128,64,128]{2,1,0:T(8,128)(2,1)S(1)} copy-done((bf16[128,64,128]{2,1,0:T(8,128)(2,1)S(1)}, bf16[128,64,128]{2,1,0:T(8,128)(2,1)}, u32[]{:S(2)}) %copy-start.2) | copy-done | bytes 2097176
  12.7 25.8 %shard_map.95 = bf16[4096,512]{1,0:T(8,128)(2,1)S(1)} custom-call(s32[128]{0:T(128)S(1)} %shift-left_add_fusion.codes, f32[54,128]{1,0:T(8,128)S(1)} %get-tuple-element.13.rows_ref, f32[54,128]{1,0:T(8,128)S(1)} %get-tuple-element.11.cols_ref, bf16[128,64,128]{2,1,0:T(8,128)(2,1)S(1)} %copy-done.2), custom_call_target="tpu_custom_call" | custom-call | flops 9663676416 | bytes 41943040 | tf_op jit(solution)/shard_map/pallas_call | solution.py:309
  38.5 0.0 copy-start
  38.5 2.0 %copy-done = bf16[4096,512]{1,0:T(8,128)(2,1)} copy-done((bf16[4096,512]{1,0:T(8,128)(2,1)}, bf16[4096,512]{1,0:T(8,128)(2,1)S(1)}, u32[]{:S(2)}) %copy-start) | copy-done | bytes 4194328
  40.5 0.0 reduce-scatter.2.cloned.1.call-update
  40.5 23.1 %all-gather.2.cloned.1.call-done.sky_ref = bf16[4096,512]{1,0:T(8,128)(2,1)} async-done(((bf16[256,512]{1,0:T(8,128)(2,1)}), bf16[4096,512]{1,0:T(8,128)(2,1)}) %all-gather.2.cloned.1.call-update) | async-done | bytes 4194320 | tf_op jit(solution)/shard_map/all_gather | solution.py:308
  63.6 0.0 copy-start.1
  63.6 2.2 %copy-done.1 = bf16[4096,512]{1,0:T(8,128)(2,1)S(1)} copy-done((bf16[4096,512]{1,0:T(8,128)(2,1)S(1)}, bf16[4096,512]{1,0:T(8,128)(2,1)}, u32[]{:S(2)}) %copy-start.1) | copy-done | bytes 4194328
  65.8 23.6 %shard_map.96 = bf16[128,64,128]{2,1,0:T(8,128)(2,1)} custom-call(s32[128]{0:T(128)S(1)} %shift-left_add_fusion.codes, f32[54,128]{1,0:T(8,128)S(1)} %get-tuple-element.12.rows_ref, f32[54,128]{1,0:T(8,128)S(1)} %get-tuple-element.10.cols_ref, bf16[4096,512]{1,0:T(8,128)(2,1)S(1)} %copy-done.1), custom_call_target="tpu_custom_call" | custom-call | flops 9663676416 | bytes 41943040 | tf_op jit(solution)/shard_map/pallas_call | solution.py:324
  89.4 49.6 %reduce-scatter.2.cloned.1.call-done = bf16[256,512]{1,0:T(8,128)(2,1)} async-done(((bf16[4096,512]{1,0:T(8,128)(2,1)}), bf16[256,512]{1,0:T(8,128)(2,1)}) %reduce-scatter.2.cloned.1.call-update) | async-done | bytes 262160 | tf_op jit(solution)/shard_map/reduce_scatter | solution.py:323
  (3 shorter events, 0.0 us)
Async XLA Ops:
  7.2 56.4 %all-gather.2.cloned.1.call-start = ((), (), s32[]{:S(2)}) async-start(), calls=%async_computation.2 | async-start | bytes 4456448 | tf_op jit(solution)/shard_map/all_gather | solution.py:308
  7.9 131.1 %reduce-scatter.2.cloned.1.call-start = ((), (), s32[]{:S(2)}) async-start(), calls=%async_computation.1 | async-start | bytes 4456448 | tf_op jit(solution)/shard_map/reduce_scatter | solution.py:323
  11.1 1.6 %copy-start.2 = (bf16[128,64,128]{2,1,0:T(8,128)(2,1)S(1)}, bf16[128,64,128]{2,1,0:T(8,128)(2,1)}, u32[]{:S(2)}) copy-start(bf16[128,64,128]{2,1,0:T(8,128)(2,1)} %stamps_ref.1) | copy-start | bytes 6291460
  38.5 2.0 %copy-start = (bf16[4096,512]{1,0:T(8,128)(2,1)}, bf16[4096,512]{1,0:T(8,128)(2,1)S(1)}, u32[]{:S(2)}) copy-start(bf16[4096,512]{1,0:T(8,128)(2,1)S(1)} %shard_map.95) | copy-start | bytes 12582916
  63.6 2.2 %copy-start.1 = (bf16[4096,512]{1,0:T(8,128)(2,1)S(1)}, bf16[4096,512]{1,0:T(8,128)(2,1)}, u32[]{:S(2)}) copy-start(bf16[4096,512]{1,0:T(8,128)(2,1)} %all-gather.2.cloned.1.call-done.sky_ref) | copy-start | bytes 12582916
Sparse Core Ops, SparseCore 0:
  10.2 53.3 all-gather.1
  68.0 70.9 reduce-scatter.1

commit v2 on v0

--- a/solution.py
+++ b/solution.py
@@ -3,6 +3,8 @@
 import jax
 import jax.numpy as jnp
 from jax import lax
+from jax.experimental import pallas as pl
+from jax.experimental.pallas import tpu as pltpu
 from jax.sharding import PartitionSpec as P
 
 
@@ -142,6 +144,361 @@
     return (tile_image, stamp_grad)
 
 
+MESH = pl.DeviceIdType.MESH
+
+
+def band_matrix(taps, lanes):
+    count = taps.shape[1]
+    half = (count - 1) // 2
+    row = jnp.concatenate([taps, jnp.zeros((1, lanes - count), jnp.float32)], axis=1)
+    spread = jnp.broadcast_to(row, (lanes, lanes))
+    turned = pltpu.roll(spread, lanes - half, 1, stride=1, stride_axis=0)
+    down = lax.broadcasted_iota(jnp.int32, (lanes, lanes), 0)
+    across = lax.broadcasted_iota(jnp.int32, (lanes, lanes), 1)
+    return jnp.where(jnp.abs(across - down) <= half, turned, 0.0)
+
+
+def build_kernel(rows_ref, cols_ref, cot_ref, row_fwd, row_bwd, col_fwd, col_bwd, blocks_ref):
+    models, terms, _ = rows_ref.shape
+    size = row_bwd.shape[1]
+    lanes = col_bwd.shape[1]
+
+    def build(m, carry):
+        taps_rows, taps_cols = rows_ref[m], cols_ref[m]
+        turned = []
+        for k in range(terms):
+            mat = band_matrix(taps_rows[k:k + 1], lanes)
+            row_fwd[m, k * size:(k + 1) * size, :] = mat[:size, :size].astype(jnp.bfloat16)
+            turned.append(mat.T[:size, :size].astype(jnp.bfloat16))
+            mat = band_matrix(taps_cols[k:k + 1], lanes)
+            col_bwd[m, :, k * lanes:(k + 1) * lanes] = mat.astype(jnp.bfloat16)
+            col_fwd[m, k * lanes:(k + 1) * lanes, :] = mat.T.astype(jnp.bfloat16)
+        row_bwd[m] = jnp.concatenate(turned, axis=1)
+        return carry
+
+    lax.fori_loop(0, models, build, 0)
+    block_count, block_rows, stamp_cols = blocks_ref.shape
+    across = cot_ref.shape[1] // stamp_cols
+    for b in range(block_count):
+        top, left = b // across * block_rows, b % across * stamp_cols
+        blocks_ref[b] = cot_ref[top:top + block_rows, left:left + stamp_cols]
+
+
+def add_kernel(model_bits, col_blocks, group, codes, conv_ref, strip_ref, total):
+    count, stamp_rows, stamp_cols = conv_ref.shape
+    block_rows = stamp_rows // 2
+    strip_rows = strip_ref.shape[0]
+
+    def clear(i, carry):
+        spot = pl.ds(pl.multiple_of(i * block_rows, block_rows), block_rows)
+        total[spot, :] = jnp.zeros((block_rows, total.shape[1]), jnp.float32)
+        return carry
+
+    lax.fori_loop(0, total.shape[0] // block_rows, clear, 0)
+
+    def some(g, carry):
+        for u in range(group):
+            block = codes[g * group + u] >> model_bits
+            top = pl.multiple_of((block // col_blocks) * block_rows, block_rows)
+            left = pl.multiple_of((block % col_blocks) * stamp_cols, stamp_cols)
+            spot = (pl.ds(top, stamp_rows), pl.ds(left, stamp_cols))
+            total[spot] = total[spot] + conv_ref[g * group + u].astype(jnp.float32)
+        return carry
+
+    lax.fori_loop(0, count // group, some, 0)
+
+    def put(i, carry):
+        spot = pl.ds(pl.multiple_of(i * block_rows, block_rows), block_rows)
+        strip_ref[spot, :] = total[spot, :].astype(jnp.bfloat16)
+        return carry
+
+    lax.fori_loop(0, strip_rows // block_rows, put, 0)
+
+
+class Place:
+    def __init__(self, peers):
+        self.planes = peers // 4
+        self.me = lax.axis_index("tile")
+        self.core = lax.rem(self.me, 2)
+        self.row = lax.rem(self.me // 2, 2)
+        self.plane = self.me // 4
+
+    def at(self, shift=0, row=0, core=0):
+        plane = lax.rem(self.plane + shift + self.planes, self.planes)
+        y = 1 - self.row if row else self.row
+        c = 1 - self.core if core else self.core
+        return plane * 4 + y * 2 + c
+
+    def greet(self):
+        barrier = pltpu.get_barrier_semaphore()
+        others = [self.at(d) for d in range(1, self.planes)] + [self.at(row=1), self.at(core=1)]
+        for other in others:
+            pl.semaphore_signal(barrier, inc=1, device_id={"tile": other}, device_id_type=MESH)
+        pl.semaphore_wait(barrier, len(others))
+
+
+def remote(src, dst, send, recv, device):
+    return pltpu.make_async_remote_copy(src_ref=src, dst_ref=dst, send_sem=send, recv_sem=recv,
+                                        device_id={"tile": device}, device_id_type=MESH)
+
+
+def forward_kernel(peers, terms, model_bits, group, codes, row_ops, col_ops, stamps_ref, cot_ref,
+                   conv_ref, sky, own_sem, z_send, z_recv, y_send, y_recv, c_send, c_recv):
+    place = Place(peers)
+    planes = place.planes
+    count, stamp_rows, stamp_cols = stamps_ref.shape
+    groups = count // group
+
+    def some(g, carry):
+        for u in range(group):
+            s = g * group + u
+            model = codes[s] & ((1 << model_bits) - 1)
+            first = jnp.dot(row_ops[model], stamps_ref[s],
+                            preferred_element_type=jnp.float32).astype(jnp.bfloat16)
+            wide = jnp.concatenate(
+                [first[k * stamp_rows:(k + 1) * stamp_rows] for k in range(terms)], axis=1)
+            conv_ref[s] = jnp.dot(wide, col_ops[model],
+                                  preferred_element_type=jnp.float32).astype(jnp.bfloat16)
+        return carry
+
+    reached = [0]
+
+    def compute(share):
+        stop = min(groups, reached[0] + share)
+        if stop > reached[0]:
+            lax.fori_loop(reached[0], stop, some, 0)
+        reached[0] = stop
+
+    place.greet()
+    own = pltpu.make_async_copy(cot_ref, sky.at[place.me], own_sem)
+    own.start()
+    to_z, to_y, to_c = {}, {}, {}
+    for d in range(1, planes):
+        to_z[d] = remote(cot_ref, sky.at[place.me], z_send.at[d], z_recv.at[d], place.at(d))
+        to_z[d].start()
+    to_y[0] = remote(cot_ref, sky.at[place.me], y_send.at[0], y_recv.at[0], place.at(row=1))
+    to_y[0].start()
+    to_c[0] = remote(cot_ref, sky.at[place.me], c_send.at[0], c_recv.at[0], place.at(core=1))
+    to_c[0].start()
+    compute(groups * 5 // 16)
+    for d in range(1, planes):
+        tile = sky.at[place.at(-d)]
+        remote(tile, tile, z_send.at[d], z_recv.at[d], place.at(d)).wait_recv()
+        to_y[d] = remote(tile, tile, y_send.at[d], y_recv.at[d], place.at(row=1))
+        to_y[d].start()
+        to_c[d] = remote(tile, tile, c_send.at[d], c_recv.at[d], place.at(core=1))
+        to_c[d].start()
+        compute(groups * 3 // 16)
+    for d in range(planes):
+        tile = sky.at[place.at(-d, row=1)]
+        e = planes + d
+        remote(tile, tile, y_send.at[d], y_recv.at[d], place.at(row=1)).wait_recv()
+        to_c[e] = remote(tile, tile, c_send.at[e], c_recv.at[e], place.at(core=1))
+        to_c[e].start()
+        compute(groups // 16 if d < planes - 1 else groups)
+    for e in range(2 * planes):
+        tile = sky.at[place.at(-(e % planes), row=e // planes, core=1)]
+        remote(tile, tile, c_send.at[e], c_recv.at[e], place.at(core=1)).wait_recv()
+    own.wait()
+    for copy in [*to_z.values(), *to_y.values(), *to_c.values()]:
+        copy.wait_send()
+
+
+def backward_kernel(peers, terms, model_bits, col_blocks, group, codes, row_ops, col_ops, sky_ref,
+                    strip, grads_ref, tile_ref, sky, from_c, out_y, from_y, out_z, from_z,
+                    own_sem, z_send, z_recv, y_send, y_recv, c_send, c_recv):
+    place = Place(peers)
+    planes = place.planes
+    count, stamp_rows, stamp_cols = grads_ref.shape
+    groups = count // group
+    block_rows = stamp_rows // 2
+    sky_blocks = sky_ref.shape[0]
+    tile_rows = tile_ref.shape[0]
+
+    def some(g, carry):
+        for u in range(group):
+            s = g * group + u
+            code = codes[s]
+            model = code & ((1 << model_bits) - 1)
+            block = code >> model_bits
+            window = jnp.concatenate([sky[block], sky[block + col_blocks]], axis=0)
+            first = jnp.dot(window, col_ops[model],
+                            preferred_element_type=jnp.float32).astype(jnp.bfloat16)
+            tall = jnp.concatenate(
+                [first[:, k * stamp_cols:(k + 1) * stamp_cols] for k in range(terms)], axis=0)
+            grads_ref[s] = jnp.dot(row_ops[model], tall,
+                                   preferred_element_type=jnp.float32).astype(jnp.bfloat16)
+        return carry
+
+    reached = [0]
+
+    def compute(share):
+        stop = min(groups, reached[0] + share)
+        if stop > reached[0]:
+            lax.fori_loop(reached[0], stop, some, 0)
+        reached[0] = stop
+
+    def summed(store, *parts):
+        def body(i, carry):
+            spot = pl.ds(pl.multiple_of(i * block_rows, block_rows), block_rows)
+            out = parts[0][0][parts[0][1], spot, :].astype(jnp.float32)
+            for ref, index in parts[1:]:
+                out = out + ref[index, spot, :].astype(jnp.float32)
+            store(spot, out.astype(jnp.bfloat16))
+            return carry
+
+        lax.fori_loop(0, tile_rows // block_rows, body, 0)
+
+    own = pltpu.make_async_copy(sky_ref, sky.at[pl.ds(0, sky_blocks)], own_sem)
+    own.start()
+    place.greet()
+    shifts = list(range(1, planes)) + [0]
+    to_c, to_y, to_z = [], [], []
+    for e in range(2 * planes):
+        far = 1 if e < planes else 0
+        source = strip.at[place.at(shifts[e % planes], row=far, core=1)]
+        to_c.append(remote(source, from_c.at[e], c_send.at[e], c_recv.at[e], place.at(core=1)))
+        to_c[-1].start()
+    sky[sky_blocks:] = jnp.zeros((col_blocks, block_rows, stamp_cols), jnp.bfloat16)
+    own.wait()
+    for i in range(planes):
+        to_c[i].wait_recv()
+
+        def keep(spot, value, i=i):
+            out_y[i, spot, :] = value
+
+        summed(keep, (strip, place.at(shifts[i], row=1)), (from_c, i))
+        to_y.append(remote(out_y.at[i], from_y.at[i], y_send.at[i], y_recv.at[i], place.at(row=1)))
+        to_y[-1].start()
+        compute(groups // 16)
+    for i in range(planes):
+        to_c[planes + i].wait_recv()
+        to_y[i].wait_recv()
+        if i == planes - 1:
+            break
+
+        def keep(spot, value, i=i):
+            out_z[i, spot, :] = value
+
+        summed(keep, (strip, place.at(shifts[i])), (from_c, planes + i), (from_y, i))
+        to_z.append(remote(out_z.at[i], from_z.at[i], z_send.at[i], z_recv.at[i],
+                           place.at(shifts[i])))
+        to_z[-1].start()
+        compute(groups * 3 // 16)
+    compute(groups)
+    for copy in to_z:
+        copy.wait_recv()
+
+    def keep(spot, value):
+        tile_ref[spot, :] = value
+
+    summed(keep, (strip, place.me), (from_c, 2 * planes - 1), (from_y, planes - 1),
+           *[(from_z, i) for i in range(planes - 1)])
+    for copy in to_c + to_y + to_z:
+        copy.wait_send()
+
+
+def divisor(number, wanted):
+    return max(d for d in range(1, wanted + 1) if number % d == 0)
+
+
+def in_place(stamps, tile_of, row_offset, col_offset, psf_model, psf_rows, psf_cols, cotangent):
+    peers = lax.axis_size("tile")
+    planes = peers // 4
+    stamp_count, stamp_rows, stamp_cols = stamps.shape
+    models, terms, taps = psf_rows.shape
+    block_rows = stamp_rows // 2
+    tile_rows, tile_cols = cotangent.shape
+    row_blocks = tile_rows // block_rows
+    col_blocks = tile_cols // stamp_cols
+    strip_rows = peers * tile_rows
+    model_bits = max(1, (models - 1).bit_length())
+    upper = tile_of[:, 0] * row_blocks + row_offset
+    codes = ((upper * col_blocks + col_offset) << model_bits) + psf_model
+    group = divisor(stamp_count, 8)
+    flops = 2 * stamp_count * terms * stamp_rows * stamp_cols * (stamp_rows + stamp_cols)
+    cost = pl.CostEstimate(flops=8 * flops, bytes_accessed=40 << 20, transcendentals=0)
+    smem = pl.BlockSpec(memory_space=pltpu.SMEM)
+    vmem = pl.BlockSpec(memory_space=pltpu.VMEM)
+    anywhere = pl.BlockSpec(memory_space=pl.ANY)
+    short = jnp.bfloat16
+    dma = pltpu.SemaphoreType.DMA
+    limit = 44 << 20
+    block_shape = (row_blocks * col_blocks, block_rows, stamp_cols)
+
+    row_fwd, row_bwd, col_fwd, col_bwd, blocks = pl.pallas_call(
+        build_kernel,
+        out_shape=(
+            jax.ShapeDtypeStruct((models, terms * stamp_rows, stamp_rows), short),
+            jax.ShapeDtypeStruct((models, stamp_rows, terms * stamp_rows), short),
+            jax.ShapeDtypeStruct((models, terms * stamp_cols, stamp_cols), short),
+            jax.ShapeDtypeStruct((models, stamp_cols, terms * stamp_cols), short),
+            jax.ShapeDtypeStruct(block_shape, short),
+        ),
+        in_specs=[vmem] * 3,
+        out_specs=(vmem,) * 5,
+        compiler_params=pltpu.CompilerParams(vmem_limit_bytes=limit),
+    )(psf_rows, psf_cols, cotangent)
+    conv, sky = pl.pallas_call(
+        partial(forward_kernel, peers, terms, model_bits, group),
+        out_shape=(
+            jax.ShapeDtypeStruct(stamps.shape, short),
+            jax.ShapeDtypeStruct((peers,) + block_shape, short),
+        ),
+        in_specs=[smem, vmem, vmem, vmem, anywhere],
+        out_specs=(vmem, anywhere),
+        scratch_shapes=[dma, dma((planes,)), dma((planes,)), dma((planes,)), dma((planes,)),
+                        dma((2 * planes,)), dma((2 * planes,))],
+        compiler_params=pltpu.CompilerParams(collective_id=0, has_side_effects=True,
+                                             vmem_limit_bytes=limit),
+        cost_estimate=cost,
+    )(codes, row_fwd, col_fwd, stamps, blocks)
+    strip = pl.pallas_call(
+        partial(add_kernel, model_bits, col_blocks, group),
+        out_shape=jax.ShapeDtypeStruct((strip_rows, tile_cols), short),
+        in_specs=[smem, vmem],
+        out_specs=vmem,
+        scratch_shapes=[pltpu.VMEM((strip_rows + block_rows, tile_cols), jnp.float32)],
+        compiler_params=pltpu.CompilerParams(vmem_limit_bytes=limit),
+    )(codes, conv)
+    tile = (tile_rows, tile_cols)
+    stamp_grad, tile_image = pl.pallas_call(
+        partial(backward_kernel, peers, terms, model_bits, col_blocks, group),
+        out_shape=(
+            jax.ShapeDtypeStruct(stamps.shape, short),
+            jax.ShapeDtypeStruct(tile, short),
+        ),
+        in_specs=[smem, vmem, vmem, anywhere, vmem],
+        out_specs=(vmem, vmem),
+        scratch_shapes=[
+            pltpu.VMEM(((peers * row_blocks + 1) * col_blocks,) + block_shape[1:], short),
+            pltpu.VMEM((2 * planes,) + tile, short),
+            pltpu.VMEM((planes,) + tile, short),
+            pltpu.VMEM((planes,) + tile, short),
+            pltpu.VMEM((planes,) + tile, short),
+            pltpu.VMEM((planes,) + tile, short),
+            dma, dma((planes,)), dma((planes,)), dma((planes,)), dma((planes,)),
+            dma((2 * planes,)), dma((2 * planes,)),
+        ],
+        compiler_params=pltpu.CompilerParams(collective_id=1, has_side_effects=True,
+                                             vmem_limit_bytes=limit),
+        cost_estimate=cost,
+    )(codes, row_bwd, col_bwd, sky.reshape((-1,) + block_shape[1:]),
+      strip.reshape((peers,) + tile))
+    return tile_image, stamp_grad
+
+
+def strip_fits(peers, cotangent):
+    rows, cols = cotangent.shape
+    return peers % 4 == 0 and peers >= 8 and peers * rows * cols * 4 <= 12 << 20
+
+
+def per_device_any(*args):
+    if strip_fits(lax.axis_size("tile"), args[-1]):
+        return in_place(*args)
+    return per_device(*args)
+
+
 def solution(mesh):
     in_specs = (
         P(("band", "tile"), None, None),
@@ -155,5 +512,5 @@
     )
     out_specs = (P(("band", "tile"), None), P(("band", "tile"), None, None))
     return jax.shard_map(
-        per_device, mesh=mesh, in_specs=in_specs, out_specs=out_specs, check_vma=False
-    )
+        per_device_any, mesh=mesh, in_specs=in_specs, out_specs=out_specs, check_vma=False
+    )

time: 208 us -> 99.9 us (0.48)
  Pallas kernels: 0 us -> 89.9 us
  starting transfers between devices: 72.5 us -> 0 us
  matrix products: 61 us -> 0 us
  local copies, waits for them, and re-layouts: 67.9 us -> 8.22 us
    pallas_call x0 -> x4, Pallas kernels: none -> 89.9 us  [the longest x1 42.7 us: in_place(): pl.pallas_call(partial(backward_kernel, peers, terms, model_bits, col_blo...]
    all_to_all x3 -> x0, starting transfers between devices: 69 us -> none  [the longest x1 56.5 us: per_device(): lax.all_to_all(for_sending(slot_grads), 'tile', split_axis=0, concat_axis...]
    dot_general x16 -> x0, matrix products: 61 us -> none  [the longest x5 26.3 us: convolve_one(): jnp.einsum('kix,kyx->iy', row_pass, col_mats, preferred_element_type=jnp....]
    gather x20 -> x0, local copies, waits for them, and re-layouts: 45 us -> none  [the longest x5 13 us: convolve_one(): col_mats = lax.dynamic_index_in_dim(col_ops, model, 0, keepdims=False)]
    another operation x8 -> x0, local copies, waits for them, and re-layouts: 13.8 us -> none  [the longest x2 5.37 us: apply_all(): return lax.map(bound, (images, models.astype(jnp.int32)), batch_size=32)]
    ppermute x2 -> x0, starting transfers between devices: 3.55 us -> none  [passed_along(): return lax.ppermute(array, axis, pairs)]
    unnamed x18 -> x12, local copies, waits for them, and re-layouts: 6.52 us -> 8.22 us
  transfers between devices with their start and end apart: 5 -> 0, of which waited for: 1 -> 0; matrix products, arithmetic and copies ran while one was open for 62% -> 0% of each run, Pallas kernels for 0% -> 0%
where the time goes in v2:
time: 99.9 us; the launch traced here: 99.6 us
  Pallas kernels  89.9 us (90%)
  local copies, waits for them, and re-layouts  8.22 us (8%)
    pallas_call x1, Pallas kernels, in_place(): pl.pallas_call(partial(backward_kernel, peers, terms, model_bits, col_blo...  42.7 us
    pallas_call x1, Pallas kernels, in_place(): pl.pallas_call(partial(forward_kernel, peers, terms, model_bits, group),...  38.9 us
    unnamed x12, local copies, waits for them, and re-layouts  8.22 us
    pallas_call x1, Pallas kernels, in_place(): pl.pallas_call(build_kernel, out_shape=(jax.ShapeDtypeStruct((models, ter...  4.79 us
    pallas_call x1, Pallas kernels, in_place(): pl.pallas_call(partial(add_kernel, model_bits, col_blocks, group), out_sh...  3.55 us

profile of v2, /device:TPU:0, one launch (start us, length us, event | category | flops | bytes accessed | tf_op | source)
XLA Modules:
  0.0 99.6 jit_solution(7303268704579992521)
XLA Ops:
  0.6 0.7 shift-left_add_fusion.codes
  1.3 0.8 copy.10.rows_ref
  2.2 0.8 copy.11.cols_ref
  3.0 0.0 copy-start.1
  3.0 0.9 copy-done.1
  4.0 4.8 %shard_map.95 = (bf16[18,192,64]{2,1,0:T(8,128)(2,1)S(1)}, bf16[18,64,192]{2,1,0:T(8,128)(2,1)S(1)}, bf16[18,384,128]{2,1,0:T(8,128)(2,1)S(1)}, bf16[18,128,384]...) custom-call(f32[18,3,15]{2,1,0:T(4,128)S(1)} %copy.10.rows_ref, f32[18,3,15]{2,1,0:T(4,128)S(1)} %copy.11.cols_ref, ...), custom_call_target="tpu_custom_call" | custom-call | tf_op jit(solution)/shard_map/pallas_call | solution.py:429
  8.8 0.0 copy-start.2
  8.8 1.6 %copy-done.2 = bf16[128,64,128]{2,1,0:T(8,128)(2,1)S(1)} copy-done((bf16[128,64,128]{2,1,0:T(8,128)(2,1)S(1)}, bf16[128,64,128]{2,1,0:T(8,128)(2,1)}, u32[]{:S(2)}) %copy-start.2) | copy-done | bytes 2097176
  10.4 38.9 %shard_map.96 = (bf16[128,64,128]{2,1,0:T(8,128)(2,1)S(1)}, bf16[16,32,32,128]{3,2,1,0:T(8,128)(2,1)}) custom-call(s32[128]{0:T(128)S(1)} %shift-left_add_fusion.codes, bf16[18,192,64]{2,1,0:T(8,128)(2,1)S(1)} %get-tuple-element.13.row_ops, bf16[18,384,128]{2,1,0:T(8,128)(2,1)S(1)} %get-tuple-element.14.col_ops, bf16[128,64,128]{2,1,0:T(8,128)(2,1)S(1)} %copy-done.2, ...), custom_call_target="tpu_custom_call" | custom-call | flops 9663676416 | bytes 41943040 | tf_op jit(solution)/shard_map/pallas_call | solution.py:442
  49.3 0.0 copy-start.3
  49.3 3.5 %shard_map.97 = bf16[4096,512]{1,0:T(8,128)(2,1)S(1)} custom-call(s32[128]{0:T(128)S(1)} %shift-left_add_fusion.codes, bf16[128,64,128]{2,1,0:T(8,128)(2,1)S(1)} %get-tuple-element.17.conv_ref), custom_call_target="tpu_custom_call" | custom-call | tf_op jit(solution)/shard_map/pallas_call | solution.py:456
  52.9 0.0 copy-start
  52.9 2.0 %copy-done = bf16[4096,512]{1,0:T(8,128)(2,1)} copy-done((bf16[4096,512]{1,0:T(8,128)(2,1)}, bf16[4096,512]{1,0:T(8,128)(2,1)S(1)}, u32[]{:S(2)}) %copy-start) | copy-done | bytes 4194328
  54.8 0.0 copy-done.3
  54.8 42.7 %shard_map.98 = (bf16[128,64,128]{2,1,0:T(8,128)(2,1)S(1)}, bf16[256,512]{1,0:T(8,128)(2,1)S(1)}) custom-call(s32[128]{0:T(128)S(1)} %shift-left_add_fusion.codes, bf16[18,64,192]{2,1,0:T(8,128)(2,1)S(1)} %get-tuple-element.11.row_ops, bf16[18,128,384]{2,1,0:T(8,128)(2,1)S(1)} %get-tuple-element.12.col_ops, bf16[512,32,128]{2,1,0:T(8,128)(2,1)S(1)} %bitcast.11, ...), custom_call_target="tpu_custom_call" | custom-call | flops 9663676416 | bytes 41943040 | tf_op jit(solution)/shard_map/pallas_call | solution.py:465
  97.5 0.7 copy.14
  98.2 1.3 %copy.15 = bf16[128,64,128]{2,1,0:T(8,128)(2,1)} copy(bf16[128,64,128]{2,1,0:T(8,128)(2,1)S(1)} %get-tuple-element.23) | data formatting | bytes 4194304
Async XLA Ops:
  3.0 0.9 copy-start.1
  8.8 1.6 %copy-start.2 = (bf16[128,64,128]{2,1,0:T(8,128)(2,1)S(1)}, bf16[128,64,128]{2,1,0:T(8,128)(2,1)}, u32[]{:S(2)}) copy-start(bf16[128,64,128]{2,1,0:T(8,128)(2,1)} %stamps_ref.1) | copy-start | bytes 6291460
  49.3 5.5 %copy-start.3 = (bf16[16,32,32,128]{3,2,1,0:T(8,128)(2,1)S(1)}, bf16[16,32,32,128]{3,2,1,0:T(8,128)(2,1)}, u32[]{:S(2)}) copy-start(bf16[16,32,32,128]{3,2,1,0:T(8,128)(2,1)} %get-tuple-element.16) | copy-start | bytes 12582916
  52.9 2.0 %copy-start = (bf16[4096,512]{1,0:T(8,128)(2,1)}, bf16[4096,512]{1,0:T(8,128)(2,1)S(1)}, u32[]{:S(2)}) copy-start(bf16[4096,512]{1,0:T(8,128)(2,1)S(1)} %shard_map.97) | copy-start | bytes 12582916

commit v3 on v2

--- a/solution.py
+++ b/solution.py
@@ -269,50 +269,85 @@
             lax.fori_loop(reached[0], stop, some, 0)
         reached[0] = stop
 
+    sky[peers] = jnp.zeros(sky.shape[1:], jnp.bfloat16)
     place.greet()
     own = pltpu.make_async_copy(cot_ref, sky.at[place.me], own_sem)
     own.start()
-    to_z, to_y, to_c = {}, {}, {}
-    for d in range(1, planes):
-        to_z[d] = remote(cot_ref, sky.at[place.me], z_send.at[d], z_recv.at[d], place.at(d))
-        to_z[d].start()
-    to_y[0] = remote(cot_ref, sky.at[place.me], y_send.at[0], y_recv.at[0], place.at(row=1))
-    to_y[0].start()
-    to_c[0] = remote(cot_ref, sky.at[place.me], c_send.at[0], c_recv.at[0], place.at(core=1))
-    to_c[0].start()
-    compute(groups * 5 // 16)
-    for d in range(1, planes):
-        tile = sky.at[place.at(-d)]
-        remote(tile, tile, z_send.at[d], z_recv.at[d], place.at(d)).wait_recv()
-        to_y[d] = remote(tile, tile, y_send.at[d], y_recv.at[d], place.at(row=1))
-        to_y[d].start()
-        to_c[d] = remote(tile, tile, c_send.at[d], c_recv.at[d], place.at(core=1))
-        to_c[d].start()
-        compute(groups * 3 // 16)
-    for d in range(planes):
-        tile = sky.at[place.at(-d, row=1)]
-        e = planes + d
-        remote(tile, tile, y_send.at[d], y_recv.at[d], place.at(row=1)).wait_recv()
-        to_c[e] = remote(tile, tile, c_send.at[e], c_recv.at[e], place.at(core=1))
-        to_c[e].start()
-        compute(groups // 16 if d < planes - 1 else groups)
-    for e in range(2 * planes):
-        tile = sky.at[place.at(-(e % planes), row=e // planes, core=1)]
-        remote(tile, tile, c_send.at[e], c_recv.at[e], place.at(core=1)).wait_recv()
+    p = place.plane
+    last = planes - 1
+
+    def z_copy(tile, source, slot, step):
+        return remote(source, sky.at[tile], z_send.at[slot], z_recv.at[slot], place.at(step))
+
+    def y_copy(tile, source, slot):
+        return remote(source, sky.at[tile], y_send.at[slot], y_recv.at[slot], place.at(row=1))
+
+    def c_copy(tile, source, slot):
+        return remote(source, sky.at[tile], c_send.at[slot], c_recv.at[slot], place.at(core=1))
+
+    def streams(i, body):
+        pl.when(p >= i)(lambda: body(-i, i, 1, p < last))
+        pl.when(p + i <= last)(lambda: body(i, last + i, -1, p > 0))
+
+    pl.when(p < last)(lambda: z_copy(place.me, cot_ref, 1, 1).start())
+    pl.when(p > 0)(lambda: z_copy(place.me, cot_ref, last + 1, -1).start())
+    y_copy(place.me, cot_ref, 0).start()
+    c_copy(place.me, cot_ref, 0).start()
+    compute(groups * 4 // 16)
+    for i in range(1, planes):
+
+        def arrived(shift, slot, step, more):
+            tile = place.at(shift)
+            source = sky.at[tile]
+            z_copy(tile, source, slot, step).wait_recv()
+            if i < last:
+                pl.when(more)(lambda: z_copy(tile, source, slot + 1, step).start())
+            y_copy(tile, source, slot).start()
+            c_copy(tile, source, slot).start()
+
+        streams(i, arrived)
+        compute(groups * 3 // 16 if i < last else groups)
+
+    half = 2 * last + 1
+
+    def crossed(shift, slot):
+        tile = place.at(shift, row=1)
+        y_copy(tile, sky.at[tile], slot).wait_recv()
+        c_copy(tile, sky.at[tile], half + slot).start()
+
+    def finished(shift, slot):
+        for row in range(2):
+            tile = place.at(shift, row=row, core=1)
+            c_copy(tile, sky.at[tile], row * half + slot).wait_recv()
+            c_copy(tile, sky.at[tile], row * half + slot).wait_send()
+        y_copy(tile, sky.at[tile], slot).wait_send()
+
+    crossed(0, 0)
+    for i in range(1, planes):
+        streams(i, lambda shift, slot, step, more: crossed(shift, slot))
+    finished(0, 0)
     own.wait()
-    for copy in [*to_z.values(), *to_y.values(), *to_c.values()]:
-        copy.wait_send()
-
-
-def backward_kernel(peers, terms, model_bits, col_blocks, group, codes, row_ops, col_ops, sky_ref,
-                    strip, grads_ref, tile_ref, sky, from_c, out_y, from_y, out_z, from_z,
-                    own_sem, z_send, z_recv, y_send, y_recv, c_send, c_recv):
+    pl.when(p < last)(lambda: z_copy(place.me, cot_ref, 1, 1).wait_send())
+    pl.when(p > 0)(lambda: z_copy(place.me, cot_ref, last + 1, -1).wait_send())
+    for i in range(1, planes):
+
+        def ended(shift, slot, step, more):
+            finished(shift, slot)
+            if i < last:
+                tile = place.at(shift)
+                pl.when(more)(lambda: z_copy(tile, sky.at[tile], slot + 1, step).wait_send())
+
+        streams(i, ended)
+
+
+def backward_kernel(peers, terms, model_bits, col_blocks, group, codes, row_ops, col_ops, sky,
+                    strip, grads_ref, tile_ref, from_c, out_y, from_y, out_z, from_z,
+                    z_send, z_recv, y_send, y_recv, c_send, c_recv):
     place = Place(peers)
     planes = place.planes
     count, stamp_rows, stamp_cols = grads_ref.shape
     groups = count // group
     block_rows = stamp_rows // 2
-    sky_blocks = sky_ref.shape[0]
     tile_rows = tile_ref.shape[0]
 
     def some(g, carry):
@@ -349,18 +384,19 @@
 
         lax.fori_loop(0, tile_rows // block_rows, body, 0)
 
-    own = pltpu.make_async_copy(sky_ref, sky.at[pl.ds(0, sky_blocks)], own_sem)
-    own.start()
     place.greet()
-    shifts = list(range(1, planes)) + [0]
-    to_c, to_y, to_z = [], [], []
+    p = place.plane
+    last = planes - 1
+    upper = p // 2
+    mirrored = (1 - 2 * upper) * p + last * upper
+    targets = [last * upper + (1 - 2 * upper) * q for q in (3, 2, 1 - mirrored, mirrored)]
+    shifts = [q - p for q in targets]
+    to_c, to_y = [], []
     for e in range(2 * planes):
         far = 1 if e < planes else 0
         source = strip.at[place.at(shifts[e % planes], row=far, core=1)]
         to_c.append(remote(source, from_c.at[e], c_send.at[e], c_recv.at[e], place.at(core=1)))
         to_c[-1].start()
-    sky[sky_blocks:] = jnp.zeros((col_blocks, block_rows, stamp_cols), jnp.bfloat16)
-    own.wait()
     for i in range(planes):
         to_c[i].wait_recv()
 
@@ -370,32 +406,56 @@
         summed(keep, (strip, place.at(shifts[i], row=1)), (from_c, i))
         to_y.append(remote(out_y.at[i], from_y.at[i], y_send.at[i], y_recv.at[i], place.at(row=1)))
         to_y[-1].start()
-        compute(groups // 16)
-    for i in range(planes):
+    compute(groups * 4 // 16)
+
+    def z_copy(i, slot, step):
+        return remote(out_z.at[i], from_z.at[slot], z_send.at[i], z_recv.at[slot], place.at(step))
+
+    for i in range(last):
         to_c[planes + i].wait_recv()
         to_y[i].wait_recv()
-        if i == planes - 1:
-            break
-
-        def keep(spot, value, i=i):
+        target = targets[i]
+        parts = [(strip, place.at(shifts[i])), (from_c, planes + i), (from_y, i)]
+
+        def keep(spot, value):
             out_z[i, spot, :] = value
 
-        summed(keep, (strip, place.at(shifts[i])), (from_c, planes + i), (from_y, i))
-        to_z.append(remote(out_z.at[i], from_z.at[i], z_send.at[i], z_recv.at[i],
-                           place.at(shifts[i])))
-        to_z[-1].start()
+        def pass_on(slot, step, first):
+            @pl.when(first)
+            def _():
+                summed(keep, *parts)
+
+            @pl.when(jnp.logical_not(first))
+            def _():
+                z_copy(i, slot, step).wait_recv()
+                summed(keep, *parts, (from_z, slot))
+
+            z_copy(i, slot, step).start()
+
+        pl.when(target > p)(lambda: pass_on(target, 1, p == 0))
+        pl.when(target < p)(lambda: pass_on(planes + target, -1, p == last))
         compute(groups * 3 // 16)
     compute(groups)
-    for copy in to_z:
-        copy.wait_recv()
-
-    def keep(spot, value):
-        tile_ref[spot, :] = value
-
-    summed(keep, (strip, place.me), (from_c, 2 * planes - 1), (from_y, planes - 1),
-           *[(from_z, i) for i in range(planes - 1)])
-    for copy in to_c + to_y + to_z:
+    to_c[2 * planes - 1].wait_recv()
+    to_y[last].wait_recv()
+    parts = [(strip, place.me), (from_c, 2 * planes - 1), (from_y, last)]
+
+    def finish(*slots):
+        for slot in slots:
+            z_copy(0, slot, 1).wait_recv()
+
+        def keep(spot, value):
+            tile_ref[spot, :] = value
+
+        summed(keep, *parts, *[(from_z, slot) for slot in slots])
+
+    pl.when(p == 0)(lambda: finish(planes + p))
+    pl.when(p == last)(lambda: finish(p))
+    pl.when(jnp.logical_and(p > 0, p < last))(lambda: finish(p, planes + p))
+    for copy in to_c + to_y:
         copy.wait_send()
+    for i in range(last):
+        z_copy(i, i, 1).wait_send()
 
 
 def divisor(number, wanted):
@@ -443,12 +503,11 @@
         partial(forward_kernel, peers, terms, model_bits, group),
         out_shape=(
             jax.ShapeDtypeStruct(stamps.shape, short),
-            jax.ShapeDtypeStruct((peers,) + block_shape, short),
+            jax.ShapeDtypeStruct((peers + 1,) + block_shape, short),
         ),
         in_specs=[smem, vmem, vmem, vmem, anywhere],
-        out_specs=(vmem, anywhere),
-        scratch_shapes=[dma, dma((planes,)), dma((planes,)), dma((planes,)), dma((planes,)),
-                        dma((2 * planes,)), dma((2 * planes,))],
+        out_specs=(vmem, vmem),
+        scratch_shapes=[dma] + [dma((2 * planes - 1,))] * 4 + [dma((4 * planes - 2,))] * 2,
         compiler_params=pltpu.CompilerParams(collective_id=0, has_side_effects=True,
                                              vmem_limit_bytes=limit),
         cost_estimate=cost,
@@ -468,16 +527,15 @@
             jax.ShapeDtypeStruct(stamps.shape, short),
             jax.ShapeDtypeStruct(tile, short),
         ),
-        in_specs=[smem, vmem, vmem, anywhere, vmem],
+        in_specs=[smem, vmem, vmem, vmem, vmem],
         out_specs=(vmem, vmem),
         scratch_shapes=[
-            pltpu.VMEM(((peers * row_blocks + 1) * col_blocks,) + block_shape[1:], short),
             pltpu.VMEM((2 * planes,) + tile, short),
             pltpu.VMEM((planes,) + tile, short),
             pltpu.VMEM((planes,) + tile, short),
             pltpu.VMEM((planes,) + tile, short),
-            pltpu.VMEM((planes,) + tile, short),
-            dma, dma((planes,)), dma((planes,)), dma((planes,)), dma((planes,)),
+            pltpu.VMEM((2 * planes,) + tile, short),
+            dma((planes,)), dma((2 * planes,)), dma((planes,)), dma((planes,)),
             dma((2 * planes,)), dma((2 * planes,)),
         ],
         compiler_params=pltpu.CompilerParams(collective_id=1, has_side_effects=True,
@@ -490,7 +548,7 @@
 
 def strip_fits(peers, cotangent):
     rows, cols = cotangent.shape
-    return peers % 4 == 0 and peers >= 8 and peers * rows * cols * 4 <= 12 << 20
+    return peers == 16 and peers * rows * cols * 4 <= 12 << 20
 
 
 def per_device_any(*args):

time: 99.9 us -> 92.1 us (0.922)
  Pallas kernels: 89.9 us -> 84.1 us
  local copies, waits for them, and re-layouts: 8.22 us -> 6.25 us
    pallas_call x1, Pallas kernels: 42.7 us -> 38.2 us  [in_place(): pl.pallas_call(partial(backward_kernel, peers, terms, model_bits, col_blo...]
    unnamed x12 -> x8, local copies, waits for them, and re-layouts: 8.22 us -> 6.25 us
    pallas_call x1, Pallas kernels: 38.9 us -> 37.6 us  [in_place(): pl.pallas_call(partial(forward_kernel, peers, terms, model_bits, group),...]
where the time goes in v3:
time: 92.1 us; the launch traced here: 91.7 us
  Pallas kernels  84.1 us (91%)
  local copies, waits for them, and re-layouts  6.25 us (7%)
    pallas_call x1, Pallas kernels, in_place(): pl.pallas_call(partial(backward_kernel, peers, terms, model_bits, col_blo...  38.2 us
    pallas_call x1, Pallas kernels, in_place(): pl.pallas_call(partial(forward_kernel, peers, terms, model_bits, group),...  37.6 us
    unnamed x8, local copies, waits for them, and re-layouts  6.25 us
    pallas_call x1, Pallas kernels, in_place(): pl.pallas_call(build_kernel, out_shape=(jax.ShapeDtypeStruct((models, ter...  4.79 us
    pallas_call x1, Pallas kernels, in_place(): pl.pallas_call(partial(add_kernel, model_bits, col_blocks, group), out_sh...  3.55 us

profile of v3, /device:TPU:0, one launch (start us, length us, event | category | flops | bytes accessed | tf_op | source)
XLA Modules:
  0.0 91.7 jit_solution(1352770407899679678)
XLA Ops:
  0.6 0.7 shift-left_add_fusion.codes
  1.3 0.8 copy.10.rows_ref
  2.2 0.8 copy.11.cols_ref
  3.0 0.0 copy-start
  3.0 0.9 %copy-done = bf16[256,512]{1,0:T(8,128)(2,1)S(1)} copy-done((bf16[256,512]{1,0:T(8,128)(2,1)S(1)}, bf16[256,512]{1,0:T(8,128)(2,1)}, u32[]{:S(2)}) %copy-start) | copy-done | bytes 262168
  4.0 4.8 %shard_map.95 = (bf16[18,192,64]{2,1,0:T(8,128)(2,1)S(1)}, bf16[18,64,192]{2,1,0:T(8,128)(2,1)S(1)}, bf16[18,384,128]{2,1,0:T(8,128)(2,1)S(1)}, bf16[18,128,384]...) custom-call(f32[18,3,15]{2,1,0:T(4,128)S(1)} %copy.10.rows_ref, f32[18,3,15]{2,1,0:T(4,128)S(1)} %copy.11.cols_ref, ...), custom_call_target="tpu_custom_call" | custom-call | tf_op jit(solution)/shard_map/pallas_call | solution.py:489
  8.8 0.0 copy-start.1
  8.8 1.6 %copy-done.1 = bf16[128,64,128]{2,1,0:T(8,128)(2,1)S(1)} copy-done((bf16[128,64,128]{2,1,0:T(8,128)(2,1)S(1)}, bf16[128,64,128]{2,1,0:T(8,128)(2,1)}, u32[]{:S(2)}) %copy-start.1) | copy-done | bytes 2097176
  10.4 37.6 %shard_map.96 = (bf16[128,64,128]{2,1,0:T(8,128)(2,1)S(1)}, bf16[17,32,32,128]{3,2,1,0:T(8,128)(2,1)}) custom-call(s32[128]{0:T(128)S(1)} %shift-left_add_fusion.codes, bf16[18,192,64]{2,1,0:T(8,128)(2,1)S(1)} %get-tuple-element.13.row_ops, bf16[18,384,128]{2,1,0:T(8,128)(2,1)S(1)} %get-tuple-element.14.col_ops, bf16[128,64,128]{2,1,0:T(8,128)(2,1)S(1)} %copy-done.1, ...), custom_call_target="tpu_custom_call" | custom-call | flops 9663676416 | bytes 41943040 | tf_op jit(solution)/shard_map/pallas_call | solution.py:502
  48.0 3.5 %shard_map.97 = bf16[4096,512]{1,0:T(8,128)(2,1)S(1)} custom-call(s32[128]{0:T(128)S(1)} %shift-left_add_fusion.codes, bf16[128,64,128]{2,1,0:T(8,128)(2,1)S(1)} %get-tuple-element.17.conv_ref), custom_call_target="tpu_custom_call" | custom-call | tf_op jit(solution)/shard_map/pallas_call | solution.py:515
  51.5 38.2 %shard_map.98 = (bf16[128,64,128]{2,1,0:T(8,128)(2,1)S(1)}, bf16[256,512]{1,0:T(8,128)(2,1)S(1)}) custom-call(s32[128]{0:T(128)S(1)} %shift-left_add_fusion.codes, bf16[18,64,192]{2,1,0:T(8,128)(2,1)S(1)} %get-tuple-element.11.row_ops, bf16[18,128,384]{2,1,0:T(8,128)(2,1)S(1)} %get-tuple-element.12.col_ops, bf16[544,32,128]{2,1,0:T(8,128)(2,1)} %bitcast.11, ...), custom_call_target="tpu_custom_call" | custom-call | flops 9663676416 | bytes 41943040 | tf_op jit(solution)/shard_map/pallas_call | solution.py:524
  89.7 0.7 copy.14
  90.4 1.3 %copy.15 = bf16[128,64,128]{2,1,0:T(8,128)(2,1)} copy(bf16[128,64,128]{2,1,0:T(8,128)(2,1)S(1)} %get-tuple-element.23) | data formatting | bytes 4194304
Async XLA Ops:
  3.0 0.9 %copy-start = (bf16[256,512]{1,0:T(8,128)(2,1)S(1)}, bf16[256,512]{1,0:T(8,128)(2,1)}, u32[]{:S(2)}) copy-start(bf16[256,512]{1,0:T(8,128)(2,1)} %cot_ref.1) | copy-start | bytes 786436
  8.8 1.6 %copy-start.1 = (bf16[128,64,128]{2,1,0:T(8,128)(2,1)S(1)}, bf16[128,64,128]{2,1,0:T(8,128)(2,1)}, u32[]{:S(2)}) copy-start(bf16[128,64,128]{2,1,0:T(8,128)(2,1)} %stamps_ref.1) | copy-start | bytes 6291460

commit v4 on v3

--- a/solution.py
+++ b/solution.py
@@ -158,13 +158,13 @@
     return jnp.where(jnp.abs(across - down) <= half, turned, 0.0)
 
 
-def build_kernel(rows_ref, cols_ref, cot_ref, row_fwd, row_bwd, col_fwd, col_bwd, blocks_ref):
-    models, terms, _ = rows_ref.shape
+def build_bands(taps_ref, row_fwd, row_bwd, col_fwd, col_bwd):
+    models, terms = taps_ref.shape[0] // 2, taps_ref.shape[1]
     size = row_bwd.shape[1]
     lanes = col_bwd.shape[1]
 
     def build(m, carry):
-        taps_rows, taps_cols = rows_ref[m], cols_ref[m]
+        taps_rows, taps_cols = taps_ref[m], taps_ref[models + m]
         turned = []
         for k in range(terms):
             mat = band_matrix(taps_rows[k:k + 1], lanes)
@@ -177,6 +177,9 @@
         return carry
 
     lax.fori_loop(0, models, build, 0)
+
+
+def into_blocks(cot_ref, blocks_ref):
     block_count, block_rows, stamp_cols = blocks_ref.shape
     across = cot_ref.shape[1] // stamp_cols
     for b in range(block_count):
@@ -242,8 +245,9 @@
                                         device_id={"tile": device}, device_id_type=MESH)
 
 
-def forward_kernel(peers, terms, model_bits, group, codes, row_ops, col_ops, stamps_ref, cot_ref,
-                   conv_ref, sky, own_sem, z_send, z_recv, y_send, y_recv, c_send, c_recv):
+def forward_kernel(peers, terms, model_bits, group, codes, taps_ref, stamps_hbm, pixels_ref,
+                   conv_ref, sky, row_bwd, col_bwd, row_ops, col_ops, stamps_ref, cot_ref,
+                   stamps_sem, own_sem, z_send, z_recv, y_send, y_recv, c_send, c_recv):
     place = Place(peers)
     planes = place.planes
     count, stamp_rows, stamp_cols = stamps_ref.shape
@@ -269,6 +273,9 @@
             lax.fori_loop(reached[0], stop, some, 0)
         reached[0] = stop
 
+    fetch = pltpu.make_async_copy(stamps_hbm, stamps_ref, stamps_sem)
+    fetch.start()
+    into_blocks(pixels_ref, cot_ref)
     sky[peers] = jnp.zeros(sky.shape[1:], jnp.bfloat16)
     place.greet()
     own = pltpu.make_async_copy(cot_ref, sky.at[place.me], own_sem)
@@ -293,7 +300,9 @@
     pl.when(p > 0)(lambda: z_copy(place.me, cot_ref, last + 1, -1).start())
     y_copy(place.me, cot_ref, 0).start()
     c_copy(place.me, cot_ref, 0).start()
-    compute(groups * 4 // 16)
+    build_bands(taps_ref, row_ops, row_bwd, col_ops, col_bwd)
+    fetch.wait()
+    compute(groups // 16)
     for i in range(1, planes):
 
         def arrived(shift, slot, step, more):
@@ -306,7 +315,7 @@
             c_copy(tile, source, slot).start()
 
         streams(i, arrived)
-        compute(groups * 3 // 16 if i < last else groups)
+        compute(groups * 4 // 16 if i < last else groups)
 
     half = 2 * last + 1
 
@@ -486,32 +495,26 @@
     limit = 44 << 20
     block_shape = (row_blocks * col_blocks, block_rows, stamp_cols)
 
-    row_fwd, row_bwd, col_fwd, col_bwd, blocks = pl.pallas_call(
-        build_kernel,
-        out_shape=(
-            jax.ShapeDtypeStruct((models, terms * stamp_rows, stamp_rows), short),
-            jax.ShapeDtypeStruct((models, stamp_rows, terms * stamp_rows), short),
-            jax.ShapeDtypeStruct((models, terms * stamp_cols, stamp_cols), short),
-            jax.ShapeDtypeStruct((models, stamp_cols, terms * stamp_cols), short),
-            jax.ShapeDtypeStruct(block_shape, short),
-        ),
-        in_specs=[vmem] * 3,
-        out_specs=(vmem,) * 5,
-        compiler_params=pltpu.CompilerParams(vmem_limit_bytes=limit),
-    )(psf_rows, psf_cols, cotangent)
-    conv, sky = pl.pallas_call(
+    conv, sky, row_bwd, col_bwd = pl.pallas_call(
         partial(forward_kernel, peers, terms, model_bits, group),
         out_shape=(
             jax.ShapeDtypeStruct(stamps.shape, short),
             jax.ShapeDtypeStruct((peers + 1,) + block_shape, short),
+            jax.ShapeDtypeStruct((models, stamp_rows, terms * stamp_rows), short),
+            jax.ShapeDtypeStruct((models, stamp_cols, terms * stamp_cols), short),
         ),
-        in_specs=[smem, vmem, vmem, vmem, anywhere],
-        out_specs=(vmem, vmem),
-        scratch_shapes=[dma] + [dma((2 * planes - 1,))] * 4 + [dma((4 * planes - 2,))] * 2,
+        in_specs=[smem, vmem, anywhere, vmem],
+        out_specs=(vmem,) * 4,
+        scratch_shapes=[
+            pltpu.VMEM((models, terms * stamp_rows, stamp_rows), short),
+            pltpu.VMEM((models, terms * stamp_cols, stamp_cols), short),
+            pltpu.VMEM(stamps.shape, short),
+            pltpu.VMEM(block_shape, short),
+        ] + [dma, dma] + [dma((2 * planes - 1,))] * 4 + [dma((4 * planes - 2,))] * 2,
         compiler_params=pltpu.CompilerParams(collective_id=0, has_side_effects=True,
                                              vmem_limit_bytes=limit),
         cost_estimate=cost,
-    )(codes, row_fwd, col_fwd, stamps, blocks)
+    )(codes, jnp.concatenate([psf_rows, psf_cols], axis=0), stamps, cotangent)
     strip = pl.pallas_call(
         partial(add_kernel, model_bits, col_blocks, group),
         out_shape=jax.ShapeDtypeStruct((strip_rows, tile_cols), short),

time: 92.1 us -> 88 us (0.955)
  Pallas kernels: 84.1 us -> 80.8 us
  local copies, waits for them, and re-layouts: 6.25 us -> 4.68 us
    pallas_call x1 -> x0, Pallas kernels: 4.79 us -> none  [in_place(): pl.pallas_call(build_kernel, out_shape=(jax.ShapeDtypeStruct((models, ter...]
    unnamed x8 -> x6, local copies, waits for them, and re-layouts: 6.25 us -> 4.56 us
    pallas_call x1, Pallas kernels: 37.6 us -> 39.1 us  [in_place(): pl.pallas_call(partial(forward_kernel, peers, terms, model_bits, group),...]
where the time goes in v4:
time: 88 us; the launch traced here: 87.7 us
  Pallas kernels  80.8 us (92%)
  local copies, waits for them, and re-layouts  4.68 us (5%)
  other arithmetic  1.54 us (2%)
    pallas_call x1, Pallas kernels, in_place(): pl.pallas_call(partial(forward_kernel, peers, terms, model_bits, group),...  39.1 us
    pallas_call x1, Pallas kernels, in_place(): pl.pallas_call(partial(backward_kernel, peers, terms, model_bits, col_blo...  38.2 us
    unnamed x6, local copies, waits for them, and re-layouts  4.56 us
    pallas_call x1, Pallas kernels, in_place(): pl.pallas_call(partial(add_kernel, model_bits, col_blocks, group), out_sh...  3.55 us

profile of v4, /device:TPU:0, one launch (start us, length us, event | category | flops | bytes accessed | tf_op | source)
XLA Modules:
  0.0 87.7 jit_solution(2819044622748137322)
XLA Ops:
  0.6 0.7 shift-left_add_fusion.codes
  1.3 0.8 pad_maximum_fusion
  2.2 0.1 copy.12.taps_ref
  2.3 0.0 copy-start
  2.3 1.6 %copy-done = bf16[128,64,128]{2,1,0:T(8,128)(2,1)S(1)} copy-done((bf16[128,64,128]{2,1,0:T(8,128)(2,1)S(1)}, bf16[128,64,128]{2,1,0:T(8,128)(2,1)}, u32[]{:S(2)}) %copy-start) | copy-done | bytes 2097176
  3.9 0.0 copy-start.1
  3.9 0.9 %copy-done.1 = bf16[256,512]{1,0:T(8,128)(2,1)S(1)} copy-done((bf16[256,512]{1,0:T(8,128)(2,1)S(1)}, bf16[256,512]{1,0:T(8,128)(2,1)}, u32[]{:S(2)}) %copy-start.1) | copy-done | bytes 262168
  4.8 39.1 %shard_map.95 = (bf16[128,64,128]{2,1,0:T(8,128)(2,1)S(1)}, bf16[17,32,32,128]{3,2,1,0:T(8,128)(2,1)}, bf16[18,64,192]{2,1,0:T(8,128)(2,1)S(1)}, bf16[18,128,384]{2,1,0:T(8,128)(2,1)S(1)}) custom-call(s32[128]{0:T(128)S(1)} %shift-left_add_fusion.codes, f32[36,3,15]{2,1,0:T(4,128)S(1)} %copy.12.taps_ref, bf16[128,64,128]{2,1,0:T(8,128)(2,1)S(1)} %copy-done, ...), custom_call_target="tpu_custom_call" | custom-call | flops 9663676416 | bytes 41943040 | tf_op jit(solution)/shard_map/pallas_call | solution.py:498
  44.0 3.5 %shard_map.96 = bf16[4096,512]{1,0:T(8,128)(2,1)S(1)} custom-call(s32[128]{0:T(128)S(1)} %shift-left_add_fusion.codes, bf16[128,64,128]{2,1,0:T(8,128)(2,1)S(1)} %get-tuple-element.11.conv_ref), custom_call_target="tpu_custom_call" | custom-call | tf_op jit(solution)/shard_map/pallas_call | solution.py:518
  47.5 38.2 %shard_map.97 = (bf16[128,64,128]{2,1,0:T(8,128)(2,1)S(1)}, bf16[256,512]{1,0:T(8,128)(2,1)S(1)}) custom-call(s32[128]{0:T(128)S(1)} %shift-left_add_fusion.codes, bf16[18,64,192]{2,1,0:T(8,128)(2,1)S(1)} %get-tuple-element.8.row_ops, bf16[18,128,384]{2,1,0:T(8,128)(2,1)S(1)} %get-tuple-element.9.col_ops, bf16[544,32,128]{2,1,0:T(8,128)(2,1)} %bitcast.11, ...), custom_call_target="tpu_custom_call" | custom-call | flops 9663676416 | bytes 41943040 | tf_op jit(solution)/shard_map/pallas_call | solution.py:527
  85.7 0.7 copy.15
  86.4 1.3 %copy.16 = bf16[128,64,128]{2,1,0:T(8,128)(2,1)} copy(bf16[128,64,128]{2,1,0:T(8,128)(2,1)S(1)} %get-tuple-element.17) | data formatting | bytes 4194304
Async XLA Ops:
  2.3 1.6 %copy-start = (bf16[128,64,128]{2,1,0:T(8,128)(2,1)S(1)}, bf16[128,64,128]{2,1,0:T(8,128)(2,1)}, u32[]{:S(2)}) copy-start(bf16[128,64,128]{2,1,0:T(8,128)(2,1)} %stamps_hbm.1) | copy-start | bytes 6291460
  3.9 0.9 %copy-start.1 = (bf16[256,512]{1,0:T(8,128)(2,1)S(1)}, bf16[256,512]{1,0:T(8,128)(2,1)}, u32[]{:S(2)}) copy-start(bf16[256,512]{1,0:T(8,128)(2,1)} %pixels_ref.1) | copy-start | bytes 786436

commit v5 on v4

--- a/solution.py
+++ b/solution.py
@@ -296,9 +296,9 @@
         pl.when(p >= i)(lambda: body(-i, i, 1, p < last))
         pl.when(p + i <= last)(lambda: body(i, last + i, -1, p > 0))
 
+    y_copy(place.me, cot_ref, 0).start()
     pl.when(p < last)(lambda: z_copy(place.me, cot_ref, 1, 1).start())
     pl.when(p > 0)(lambda: z_copy(place.me, cot_ref, last + 1, -1).start())
-    y_copy(place.me, cot_ref, 0).start()
     c_copy(place.me, cot_ref, 0).start()
     build_bands(taps_ref, row_ops, row_bwd, col_ops, col_bwd)
     fetch.wait()
@@ -315,7 +315,7 @@
             c_copy(tile, source, slot).start()
 
         streams(i, arrived)
-        compute(groups * 4 // 16 if i < last else groups)
+        compute(groups * 3 // 16 if i < last else groups)
 
     half = 2 * last + 1
 

time: 88 us -> 90.7 us (1.031)
  Pallas kernels: 80.8 us -> 83.5 us
    pallas_call x1, Pallas kernels: 39.1 us -> 41.8 us  [in_place(): pl.pallas_call(partial(forward_kernel, peers, terms, model_bits, group),...]
where the time goes in v5:
time: 90.7 us; the launch traced here: 90.4 us
  Pallas kernels  83.5 us (92%)
  local copies, waits for them, and re-layouts  4.68 us (5%)
  other arithmetic  1.54 us (2%)
    pallas_call x1, Pallas kernels, in_place(): pl.pallas_call(partial(forward_kernel, peers, terms, model_bits, group),...  41.8 us
    pallas_call x1, Pallas kernels, in_place(): pl.pallas_call(partial(backward_kernel, peers, terms, model_bits, col_blo...  38.2 us
    unnamed x6, local copies, waits for them, and re-layouts  4.56 us
    pallas_call x1, Pallas kernels, in_place(): pl.pallas_call(partial(add_kernel, model_bits, col_blocks, group), out_sh...  3.55 us

profile of v5, /device:TPU:0, one launch (start us, length us, event | category | flops | bytes accessed | tf_op | source)
XLA Modules:
  0.0 90.4 jit_solution(15276880140989737471)
XLA Ops:
  0.6 0.7 shift-left_add_fusion.codes
  1.3 0.8 pad_maximum_fusion
  2.2 0.1 copy.12.taps_ref
  2.3 0.0 copy-start
  2.3 1.6 %copy-done = bf16[128,64,128]{2,1,0:T(8,128)(2,1)S(1)} copy-done((bf16[128,64,128]{2,1,0:T(8,128)(2,1)S(1)}, bf16[128,64,128]{2,1,0:T(8,128)(2,1)}, u32[]{:S(2)}) %copy-start) | copy-done | bytes 2097176
  3.9 0.0 copy-start.1
  3.9 0.9 %copy-done.1 = bf16[256,512]{1,0:T(8,128)(2,1)S(1)} copy-done((bf16[256,512]{1,0:T(8,128)(2,1)S(1)}, bf16[256,512]{1,0:T(8,128)(2,1)}, u32[]{:S(2)}) %copy-start.1) | copy-done | bytes 262168
  4.8 41.8 %shard_map.95 = (bf16[128,64,128]{2,1,0:T(8,128)(2,1)S(1)}, bf16[17,32,32,128]{3,2,1,0:T(8,128)(2,1)}, bf16[18,64,192]{2,1,0:T(8,128)(2,1)S(1)}, bf16[18,128,384]{2,1,0:T(8,128)(2,1)S(1)}) custom-call(s32[128]{0:T(128)S(1)} %shift-left_add_fusion.codes, f32[36,3,15]{2,1,0:T(4,128)S(1)} %copy.12.taps_ref, bf16[128,64,128]{2,1,0:T(8,128)(2,1)S(1)} %copy-done, ...), custom_call_target="tpu_custom_call" | custom-call | flops 9663676416 | bytes 41943040 | tf_op jit(solution)/shard_map/pallas_call | solution.py:498
  46.6 3.5 %shard_map.96 = bf16[4096,512]{1,0:T(8,128)(2,1)S(1)} custom-call(s32[128]{0:T(128)S(1)} %shift-left_add_fusion.codes, bf16[128,64,128]{2,1,0:T(8,128)(2,1)S(1)} %get-tuple-element.11.conv_ref), custom_call_target="tpu_custom_call" | custom-call | tf_op jit(solution)/shard_map/pallas_call | solution.py:518
  50.2 38.2 %shard_map.97 = (bf16[128,64,128]{2,1,0:T(8,128)(2,1)S(1)}, bf16[256,512]{1,0:T(8,128)(2,1)S(1)}) custom-call(s32[128]{0:T(128)S(1)} %shift-left_add_fusion.codes, bf16[18,64,192]{2,1,0:T(8,128)(2,1)S(1)} %get-tuple-element.8.row_ops, bf16[18,128,384]{2,1,0:T(8,128)(2,1)S(1)} %get-tuple-element.9.col_ops, bf16[544,32,128]{2,1,0:T(8,128)(2,1)} %bitcast.11, ...), custom_call_target="tpu_custom_call" | custom-call | flops 9663676416 | bytes 41943040 | tf_op jit(solution)/shard_map/pallas_call | solution.py:527
  88.4 0.7 copy.15
  89.1 1.3 %copy.16 = bf16[128,64,128]{2,1,0:T(8,128)(2,1)} copy(bf16[128,64,128]{2,1,0:T(8,128)(2,1)S(1)} %get-tuple-element.17) | data formatting | bytes 4194304
Async XLA Ops:
  2.3 1.6 %copy-start = (bf16[128,64,128]{2,1,0:T(8,128)(2,1)S(1)}, bf16[128,64,128]{2,1,0:T(8,128)(2,1)}, u32[]{:S(2)}) copy-start(bf16[128,64,128]{2,1,0:T(8,128)(2,1)} %stamps_hbm.1) | copy-start | bytes 6291460
  3.9 0.9 %copy-start.1 = (bf16[256,512]{1,0:T(8,128)(2,1)S(1)}, bf16[256,512]{1,0:T(8,128)(2,1)}, u32[]{:S(2)}) copy-start(bf16[256,512]{1,0:T(8,128)(2,1)} %pixels_ref.1) | copy-start | bytes 786436
